TPU v7x, 32 devices: a whole 2x2x4 slice. The times are simulated.
32 devices in a mesh: rep: 4 (over x, core), exp: 8 (over z, y).
Axes of the slice: x: 2, y: 2, z: 4, core: 2. Of those that a mesh axis runs over, the one named last changes fastest.
Arguments:
- inputs: bfloat16 [4096, 2048], P(('rep', 'exp')), may hold values from -6 to 6
- out_grad: bfloat16 [4096, 2048], P(('rep', 'exp')), may hold values from -6 to 6
- routes: int32 [4096, 8], P(('rep', 'exp')), may hold values from 0 to 63, all different within a row; in each aligned block of 128 rows (0 to 127, 128 to 255, ...) at most 18 rows name the same one
- gates: float32 [4096, 8], P(('rep', 'exp')), may hold values from 0.05 to 0.3
- weights: bfloat16 [2048, 64, 3, 384], P('rep', 'exp'), may hold values from -0.125 to 0.125
- moment_one: float32 [2048, 64, 3, 384], P('rep', 'exp'), may hold values from -18 to 18
- moment_two: float32 [2048, 64, 3, 384], P('rep', 'exp'), may hold values from 1 to 100
Outputs:
- input_grad: bfloat16 [4096, 2048], P(('rep', 'exp'))
- first_moment: float32 [2048, 64, 3, 384], P('rep', 'exp')
- second_moment: float32 [2048, 64, 3, 384], P('rep', 'exp')
- new_weights: bfloat16 [2048, 64, 3, 384], P('rep', 'exp')
Inputs may be any that keep to these rules, and one draw needn't show every extreme that they name: `routes`: each row names 8 different experts. In the rows of one device no expert is named by more than 18 rows, a bound that some block reaches.
All inputs are finite; a program needn't handle non-finite values.
Results may differ from a plain program's by a relative error of at most 0.0064.
Values may be sent and summed in bfloat16 or wider, within the bound.
A program may use at most 384 MiB of HBM per device.

v0:
```python
import functools

import jax
import jax.numpy as jnp
from jax import lax
from jax.experimental import pallas as pl
from jax.experimental.pallas import tpu as pltpu
from jax.sharding import PartitionSpec as P


CAP = 18


beta_one = 0.9
beta_two = 0.95
learn_rate = 0.002
decay_rate = 0.1
epsilon = 1e-08
step_count = 100

F32 = jnp.float32
BF16 = jnp.bfloat16


def update_kernel(dims, *refs):
    (replicas, slots, part, local, kinds, ffn, block, depth, _) = dims
    pieces, refs = refs[:4], refs[4:]
    m_one, m_two, w_in, o_one, o_two, w_out = refs[:6]
    bufs, (grad, b_one, b_two, b_w, in_sem, load_sem, store_sem) = refs[6:10], refs[10:]
    rows = replicas * slots
    twin = min(2, local)
    blocks = part // block
    ahead = min(depth, blocks)
    lanes = grad.shape[2]

    def fetch(e, go):
        for kind in range(4):
            for q in range(replicas):
                n = kind * replicas + q
                copy = pltpu.make_async_copy(
                    pieces[kind].at[q, e],
                    bufs[kind].at[lax.rem(e, twin), pl.ds(q * slots, slots)],
                    in_sem.at[lax.rem(e, twin), n],
                )
                copy.start() if go else copy.wait()

    def moves(i, outward):
        s = lax.rem(i, depth)
        part_of = pl.ds(i * block, block)
        if outward:
            trio = ((b_one, o_one), (b_two, o_two), (b_w, w_out))
            return [
                pltpu.make_async_copy(a.at[s], b.at[part_of], store_sem.at[n, s])
                for n, (a, b) in enumerate(trio)
            ]
        trio = ((b_one, m_one), (b_two, m_two), (b_w, w_in))
        return [
            pltpu.make_async_copy(b.at[part_of], a.at[s], load_sem.at[n, s])
            for n, (a, b) in enumerate(trio)
        ]

    fetch(0, True)

    @pl.loop(0, ahead)
    def _(i):
        for copy in moves(i, False):
            copy.start()

    @pl.loop(0, local)
    def _(e):
        if twin > 1:

            @pl.when(e + 1 < local)
            def _():
                fetch(e + 1, True)

        fetch(e, False)
        at = lax.rem(e, twin)
        base = pl.multiple_of(e * part, part)
        step = rows if rows <= 1024 else slots
        for lead, width, left, right in ((0, 2 * ffn, 0, 2), (2 * ffn, ffn, 1, 3)):
            for start in range(0, rows, step):
                one = lax.dot_general(
                    bufs[left][at, pl.ds(start, step), :],
                    bufs[right][at, pl.ds(start, step), :],
                    (((0,), (0,)), ((), ())),
                    preferred_element_type=F32,
                )
                for c in range(width // lanes):
                    tile = one[:, c * lanes : (c + 1) * lanes]
                    place = lead // lanes + c
                    if start:
                        tile = tile + grad[place, pl.ds(base, part), :]
                    grad[place, pl.ds(base, part), :] = tile

    correct_one = 1.0 - beta_one**step_count
    correct_two = 1.0 - beta_two**step_count

    @pl.loop(0, blocks)
    def _(i):
        s = lax.rem(i, depth)
        for copy in moves(i, False):
            copy.wait()

        @pl.loop(0, block // 4)
        def _(pair):
            spots = []
            for sub in range(4):
                row = pair * 4 + sub
                d = i * block + row
                of_d = pl.ds(d, local, stride=part) if local > 1 else pl.ds(d, 1)
                for place in range(kinds * ffn // lanes):
                    kind, c = divmod(place * lanes, ffn)
                    spots.append(((s, row, kind, slice(None), pl.ds(c, lanes)), place, of_d))
            held = [(b_one[at], b_two[at], b_w[at], grad[place, of_d, :]) for at, place, of_d in spots]
            done = []
            for one, two, w, g in held:
                first = beta_one * one + (1.0 - beta_one) * g
                second = beta_two * two + (1.0 - beta_two) * g * g
                w = w.astype(F32)
                root = jnp.sqrt(second * (1.0 / correct_two)) + epsilon
                update = first * (1.0 / correct_one) / root + decay_rate * w
                done.append((first, second, (w - learn_rate * update).astype(BF16)))
            for (at, _, _), (first, second, new) in zip(spots, done):
                b_one[at] = first
                b_two[at] = second
                b_w[at] = new

        for copy in moves(i, True):
            copy.start()

        @pl.when((i >= 1) & (i - 1 + depth < blocks))
        def _():
            for copy in moves(i - 1, True):
                copy.wait()
            for copy in moves(i - 1 + depth, False):
                copy.start()

    @pl.loop(max(blocks - depth, 0), blocks)
    def _(i):
        for copy in moves(i, True):
            copy.wait()


def expert_update(rows_x, rows_g, d_pair, acts, weights, moment_one, moment_two):
    replicas, local, slots, part = rows_x.shape
    kinds, ffn = weights.shape[2:]
    block = 32
    twin = min(2, local)
    rows = replicas * slots
    pieces = (rows_x, rows_g, d_pair, acts)
    held = [a.transpose(0, 2, 1, 3) for a in (moment_one, moment_two, weights)]
    depth = 10
    any_spec = pl.BlockSpec(memory_space=pl.ANY)
    kernel = functools.partial(
        update_kernel, (replicas, slots, part, local, kinds, ffn, block, depth, None)
    )
    outs = pl.pallas_call(
        kernel,
        out_shape=tuple(jax.ShapeDtypeStruct(a.shape, a.dtype) for a in held),
        in_specs=[any_spec] * (len(pieces) + 3),
        out_specs=(any_spec,) * 3,
        scratch_shapes=[
            pltpu.VMEM((twin, rows, part), BF16),
            pltpu.VMEM((twin, rows, part), BF16),
            pltpu.VMEM((twin, rows, 2 * ffn), BF16),
            pltpu.VMEM((twin, rows, ffn), BF16),
            pltpu.VMEM((kinds * ffn // 128, local * part, 128), F32),
            pltpu.VMEM((depth, block, kinds, local, ffn), F32),
            pltpu.VMEM((depth, block, kinds, local, ffn), F32),
            pltpu.VMEM((depth, block, kinds, local, ffn), BF16),
            pltpu.SemaphoreType.DMA((twin, 4 * replicas)),
            pltpu.SemaphoreType.DMA((3, depth)),
            pltpu.SemaphoreType.DMA((3, depth)),
        ],
        compiler_params=pltpu.CompilerParams(vmem_limit_bytes=60 << 20),
        cost_estimate=pl.CostEstimate(
            flops=2 * rows * part * kinds * ffn * local,
            bytes_accessed=2 * sum(a.size * a.dtype.itemsize for a in held),
            transcendentals=0,
        ),
        name="expert_update",
    )(*pieces, *held)
    return [a.transpose(0, 2, 1, 3) for a in outs]


MESH = pl.DeviceIdType.MESH


def flip(index, bits):
    for bit in (1, 2):
        if bits & bit:
            index = index + bit * (1 - 2 * ((index // bit) % 2))
    return index


def forward_kernel(dims, x, g, meta, weights, out_x, out_g, out_pair, out_act, out_rank, *scratch):
    replicas, sources, tok, part, local, slots, ffn, cap = dims
    (gx, gg, gm, w, rank, gate, rows_x, rows_g, outgoing, incoming, own, held, raw, turned) = scratch[:14]
    (own_send, got, sent, w_sem, part_send, part_got, d_send, d_got, out_sem) = scratch[14:]
    me, ex = lax.axis_index("rep"), lax.axis_index("exp")
    col, z = ex % 2, ex // 2
    line = sources // 2
    side = ex + 1 - 2 * col
    above, below = z + 1 < line, z >= 1
    pair = 2 * ffn
    order = tuple(reversed(range(replicas)))
    kinds = ((gm, meta), (gx, x), (gg, g))

    barrier = pltpu.get_barrier_semaphore()
    for q in order[:-1]:
        pl.semaphore_signal(barrier, inc=1, device_id={"rep": flip(me, q)}, device_id_type=MESH)
    pl.semaphore_signal(barrier, inc=1, device_id={"exp": side}, device_id_type=MESH)

    @pl.when(above)
    def _():
        pl.semaphore_signal(barrier, inc=1, device_id={"exp": ex + 2}, device_id_type=MESH)

    @pl.when(below)
    def _():
        pl.semaphore_signal(barrier, inc=1, device_id={"exp": ex - 2}, device_id_type=MESH)

    lanes = turned.shape[2]
    chunk = raw.shape[1]
    chunks = part // chunk

    def load_w(c):
        return pltpu.make_async_copy(
            weights.at[pl.ds(c * chunk, chunk)], raw.at[c % 2], w_sem.at[c % 2]
        )

    def turn(c):
        if c + 1 < chunks:
            load_w(c + 1).start()
        load_w(c).wait()
        unroll = 4

        @pl.loop(0, chunk // unroll)
        def _(d4):
            for sub in range(unroll):
                d = d4 * unroll + sub
                for place in range(3 * ffn // lanes):
                    kind, at = divmod(place * lanes, ffn)
                    tile = raw[c % 2, d, kind, :, pl.ds(at, lanes)].astype(F32)
                    turned[place, pl.ds(d, local, stride=chunk), :] = tile

        @pl.loop(0, local)
        def _(l):
            for place in range(3 * ffn // lanes):
                tile = turned[place, pl.ds(pl.multiple_of(l * chunk, chunk), chunk), :]
                w[l, pl.ds(c * chunk, chunk), pl.ds(place * lanes, lanes)] = tile.astype(BF16)

    load_w(0).start()
    expected = replicas + jnp.where(above, 1, 0) + jnp.where(below, 1, 0)
    pl.semaphore_wait(barrier, expected)

    def first(q, n):
        buf, src = kinds[n]
        target = flip(me, q)
        if n:
            src = src.at[:, pl.ds(pl.multiple_of(target * part, part), part)]
        if q == 0:
            return pltpu.make_async_copy(src, buf.at[q, ex], got.at[q, n, ex])
        return pltpu.make_async_remote_copy(
            src_ref=src,
            dst_ref=buf.at[q, ex],
            send_sem=own_send.at[q, n],
            recv_sem=got.at[q, n, ex],
            device_id={"rep": target},
            device_id_type=MESH,
        )

    def hop(q, n, slot, way):
        target = (side, ex + 2, ex - 2)[way]
        return pltpu.make_async_remote_copy(
            src_ref=kinds[n][0].at[q, slot],
            dst_ref=kinds[n][0].at[q, slot],
            send_sem=sent.at[way, q, n, slot],
            recv_sem=got.at[q, n, slot],
            device_id={"exp": target},
            device_id_type=MESH,
        )

    for q in order:
        for n in range(3):
            first(q, n).start()

    def relay(q, step):
        for n in range(3):
            if step == 0:
                if q:
                    first(q, n).wait_recv()
                else:
                    first(q, n).wait()
                hop(q, n, ex, 0).start()

                @pl.when(above)
                def _():
                    hop(q, n, ex, 1).start()

                @pl.when(below)
                def _():
                    hop(q, n, ex, 2).start()

                continue

            @pl.when(z >= step)
            def _():
                slot = ex - 2 * step
                hop(q, n, slot, 0).wait_recv()
                hop(q, n, slot, 0).start()

                @pl.when(above)
                def _():
                    hop(q, n, slot, 1).start()

            @pl.when(z + step < line)
            def _():
                slot = ex + 2 * step
                hop(q, n, slot, 0).wait_recv()
                hop(q, n, slot, 0).start()

                @pl.when(below)
                def _():
                    hop(q, n, slot, 2).start()

    def settle(q):
        for n in range(3):
            for level in range(line):
                hop(q, n, 2 * level + 1 - col, 0).wait_recv()

    lower = lax.broadcasted_iota(jnp.int32, (tok, tok), 0)
    upper = lax.broadcasted_iota(jnp.int32, (tok, tok), 1)
    earlier = jnp.where(lower < upper, 1.0, 0.0).astype(BF16)
    expert0 = (ex * local).astype(F32)

    def prepare(q):
        @pl.loop(0, sources)
        def _(s):
            info = gm[q, s].astype(F32)[:8]
            routes = info[:, :tok]
            weight = info[:, tok : 2 * tok] + info[:, 2 * tok : 3 * tok] + info[:, 3 * tok :]
            named, gates = [], []
            for l in range(local):
                hit = routes == expert0 + l
                named.append(jnp.max(jnp.where(hit, 1.0, 0.0), axis=0, keepdims=True))
                gates.append(jnp.sum(jnp.where(hit, weight, 0.0), axis=0, keepdims=True))
            named = jnp.concatenate(named, axis=0)
            places = jnp.dot(named.astype(BF16), earlier, preferred_element_type=F32)
            places = jnp.where(named > 0.0, places + (s * cap).astype(F32), -1.0)
            at = pl.ds(pl.multiple_of(s * tok, tok), tok)
            rank[q, :, at] = places
            gate[:, at] = jnp.concatenate(gates, axis=0)

    def exchange(l, q):
        slot, into, bits = {3: (0, 0, 1), 2: (1, 2, 2), 1: (0, 1, 1)}[q]
        return pltpu.make_async_remote_copy(
            src_ref=outgoing.at[slot, l],
            dst_ref=incoming.at[into, l],
            send_sem=part_send.at[q, l],
            recv_sem=part_got.at[into, l],
            device_id={"rep": flip(me, bits)},
            device_id_type=MESH,
        )

    def row_out(l, q):
        return (
            pltpu.make_async_copy(rows_x.at[q, l], out_x.at[q, l], out_sem.at[0, q, l]),
            pltpu.make_async_copy(rows_g.at[q, l], out_g.at[q, l], out_sem.at[1, q, l]),
        )

    def piece(l, q):
        places = rank[q, pl.ds(l, 1), :]
        index = lax.broadcasted_iota(jnp.int32, (slots, sources * tok), 0).astype(F32)
        hit = index == places
        pick = jnp.where(hit, 1.0, 0.0).astype(BF16)
        gates = jnp.sum(jnp.where(hit, gate[pl.ds(l, 1), :], 0.0), axis=1, keepdims=True)
        tokens_x = gx[q].reshape(sources * tok, part)
        tokens_g = gg[q].reshape(sources * tok, part)
        rx = jnp.dot(pick, tokens_x, preferred_element_type=F32).astype(BF16)
        rg = (jnp.dot(pick, tokens_g, preferred_element_type=F32) * gates).astype(BF16)
        rows_x[q, l] = rx
        rows_g[q, l] = rg
        for copy in row_out(l, q):
            copy.start()
        hidden = jnp.dot(rx, w[l, :, :pair], preferred_element_type=F32)
        da = jnp.dot(rg, w[l, :, pair:], preferred_element_type=F32)
        for lead, width, one in ((0, pair, hidden), (pair, ffn, da)):
            at = pl.ds(lead, width)
            if q == 3:
                outgoing[0, l, :, at] = one.astype(BF16)
            elif q == 2:
                if not lead:
                    exchange(l, 3).wait_recv()
                outgoing[1, l, :, at] = (one + incoming[0, l, :, at].astype(F32)).astype(BF16)
            elif q == 1:
                if not lead:
                    exchange(l, 3).wait_send()
                outgoing[0, l, :, at] = one.astype(BF16)
            else:
                if not lead:
                    exchange(l, 1).wait_recv()
                own[l, :, at] = one + incoming[1, l, :, at].astype(F32)
        if q:
            exchange(l, q).start()

    def grads_to(l, way):
        src, dst, bits = ((0, 1, 1), (0, 2, 2), (2, 3, 1))[way]
        return pltpu.make_async_remote_copy(
            src_ref=held.at[src, l],
            dst_ref=held.at[dst, l],
            send_sem=d_send.at[way, l],
            recv_sem=d_got.at[way, l],
            device_id={"rep": flip(me, bits)},
            device_id_type=MESH,
        )

    def d_out(l, q):
        return (
            pltpu.make_async_copy(
                held.at[q, l, :, pl.ds(0, pair)], out_pair.at[q, l], out_sem.at[2, q, l]
            ),
            pltpu.make_async_copy(
                held.at[q, l, :, pl.ds(pair, ffn)], out_act.at[q, l], out_sem.at[3, q, l]
            ),
        )

    def finish(l):
        exchange(l, 2).wait_recv()
        sums = [
            own[l, :, pl.ds(n * ffn, ffn)] + incoming[2, l, :, pl.ds(n * ffn, ffn)].astype(F32)
            for n in range(3)
        ]
        hg, hu, da = sums
        sig = jax.nn.sigmoid(hg)
        held[0, l, :, pl.ds(2 * ffn, ffn)] = (hg * sig * hu).astype(BF16)
        held[0, l, :, pl.ds(ffn, ffn)] = (da * hg * sig).astype(BF16)
        held[0, l, :, pl.ds(0, ffn)] = (da * hu * sig * (1.0 + hg * (1.0 - sig))).astype(BF16)
        for way in (1, 0):
            grads_to(l, way).start()
        for copy in d_out(l, 0):
            copy.start()

    def pass_on(l):
        grads_to(l, 1).wait_recv()
        grads_to(l, 2).start()
        for copy in d_out(l, 2):
            copy.start()

    def pieces(lo, hi, q):
        @pl.loop(lo, hi)
        def _(l):
            piece(l, q)

    steps = max(line - 1, 1)
    turns = [range(chunks * n // (steps + 1), chunks * (n + 1) // (steps + 1)) for n in range(steps + 1)]
    for c in turns[0]:
        turn(c)
    relay(order[0], 0)
    for i, q in enumerate(order):
        if i + 1 < replicas:
            relay(order[i + 1], 0)
        for step in range(1, line):
            relay(q, step)
            if not i:
                for c in turns[step]:
                    turn(c)
            if i:
                pieces(local * (step - 1) // steps, local * step // steps, order[i - 1])
        settle(q)
        prepare(q)

    @pl.loop(0, local + 2)
    def _(l):
        @pl.when(l < local)
        def _():
            piece(l, order[-1])
            finish(l)

        @pl.when(l >= 2)
        def _():
            pass_on(l - 2)

    rank_copy = pltpu.make_async_copy(rank, out_rank, w_sem.at[0])
    rank_copy.start()

    @pl.loop(0, local)
    def _(l):
        grads_to(l, 0).wait_recv()
        for copy in d_out(l, 1):
            copy.start()
        grads_to(l, 2).wait_recv()
        for copy in d_out(l, 3):
            copy.start()

    rank_copy.wait()

    @pl.loop(0, local)
    def _(l):
        for q in (2, 1):
            exchange(l, q).wait_send()
        for way in range(3):
            grads_to(l, way).wait_send()
        for q in range(replicas):
            for copy in row_out(l, q) + d_out(l, q):
                copy.wait()

    for q in order:
        for n in range(3):
            if q:
                first(q, n).wait_send()

            @pl.loop(0, line)
            def _(level):
                slot = 2 * level + col
                hop(q, n, slot, 0).wait_send()

                @pl.when(above & (level <= z))
                def _():
                    hop(q, n, slot, 1).wait_send()

                @pl.when(below & (level >= z))
                def _():
                    hop(q, n, slot, 2).wait_send()


def forward(inputs, out_grad, meta, weights, replicas, sources, cap):
    tok = inputs.shape[0]
    part, local, kinds, ffn = weights.shape
    width = kinds * ffn
    chunk = part // 8
    slots = sources * cap
    dims = (replicas, sources, tok, part, local, slots, ffn, cap)
    any_spec = pl.BlockSpec(memory_space=pl.ANY)
    rows = (replicas, local, slots)
    dma = pltpu.SemaphoreType.DMA
    return pl.pallas_call(
        functools.partial(forward_kernel, dims),
        out_shape=(
            jax.ShapeDtypeStruct((*rows, part), BF16),
            jax.ShapeDtypeStruct((*rows, part), BF16),
            jax.ShapeDtypeStruct((*rows, 2 * ffn), BF16),
            jax.ShapeDtypeStruct((*rows, ffn), BF16),
            jax.ShapeDtypeStruct((replicas, local, sources * tok), F32),
        ),
        in_specs=[any_spec] * 4,
        out_specs=(any_spec,) * 5,
        scratch_shapes=[
            pltpu.VMEM((replicas, sources, tok, part), BF16),
            pltpu.VMEM((replicas, sources, tok, part), BF16),
            pltpu.VMEM((replicas, sources, *meta.shape), BF16),
            pltpu.VMEM((local, part, width), BF16),
            pltpu.VMEM((replicas, local, sources * tok), F32),
            pltpu.VMEM((local, sources * tok), F32),
            pltpu.VMEM((*rows, part), BF16),
            pltpu.VMEM((*rows, part), BF16),
            pltpu.VMEM((2, local, slots, width), BF16),
            pltpu.VMEM((3, local, slots, width), BF16),
            pltpu.VMEM((local, slots, width), F32),
            pltpu.VMEM((*rows, width), BF16),
            pltpu.VMEM((2, chunk, kinds, local, ffn), BF16),
            pltpu.VMEM((width // 128, local * chunk, 128), F32),
            dma((replicas, 3)),
            dma((replicas, 3, sources)),
            dma((3, replicas, 3, sources)),
            dma((2,)),
            dma((replicas, local)),
            dma((3, local)),
            dma((3, local)),
            dma((3, local)),
            dma((4, replicas, local)),
        ],
        compiler_params=pltpu.CompilerParams(
            collective_id=0, has_side_effects=True, vmem_limit_bytes=63 << 20
        ),
        name="gather_forward",
    )(inputs, out_grad, meta, weights.transpose(0, 2, 1, 3))


def by_collectives(inputs, out_grad, terms, mats, top, sources, half, swap):
    replicas = lax.axis_size("rep")
    me = lax.axis_index("rep")
    tok_dev = inputs.shape[0]
    local, part, width = mats.shape
    ffn = width // 3
    pair = 2 * ffn
    slots = sources * CAP
    meta = jnp.concatenate(terms).reshape(-1, part)
    meta_rows = meta.shape[0]
    pad = -meta_rows % 16
    meta = jnp.pad(meta, ((0, pad), (0, 0)))

    def arrive(q):
        at = (me ^ q) * part
        x = lax.dynamic_slice_in_dim(inputs, at, part, 1)
        g = lax.dynamic_slice_in_dim(out_grad, at, part, 1)
        return swap(jnp.concatenate([x, g, meta]), q)

    gathered = {}
    for start in range(replicas - half, -1, -half):
        chosen = range(start, start + half)
        block = jnp.stack([arrive(q) for q in reversed(chosen)])
        block = lax.all_gather(block, "exp", axis=0, tiled=False)
        for place, q in enumerate(reversed(chosen)):
            gathered[q] = block[:, place]

    mine = lax.axis_index("exp") * local + jnp.arange(local, dtype=jnp.int32)
    earlier = jnp.arange(tok_dev)[:, None] < jnp.arange(tok_dev)[None, :]
    base = (jnp.arange(sources) * CAP).astype(F32)
    pair_mats, down_mats = mats[..., :pair], mats[..., pair:]
    picks, rows_x, rows_g, arrivals = {}, {}, {}, {}
    for q in reversed(range(replicas)):
        if q == half - 1 and replicas > 1:
            later = {p: gathered[p] for p in range(half)}
            later, _ = lax.optimization_barrier((later, sent))
            gathered.update(later)
        got = gathered[q]
        info = got[:, 2 * tok_dev : 2 * tok_dev + meta_rows].astype(F32)
        info = info.reshape(sources, 4, top, tok_dev)
        weight = info[:, 1] + info[:, 2] + info[:, 3]
        hit = info[:, 0][None] == mine.astype(F32)[:, None, None, None]
        named = jnp.any(hit, axis=2)
        gate = jnp.sum(jnp.where(hit, weight[None], 0.0), axis=2)
        rank = jnp.einsum(
            "let,tu->leu", named.astype(BF16), earlier.astype(BF16), preferred_element_type=F32
        )
        rank = jnp.where(named, rank + base[None, :, None], -1.0)
        rank = rank.reshape(local, 1, sources * tok_dev)
        onehot = rank == jnp.arange(slots, dtype=F32)[None, :, None]
        gate = gate.reshape(local, 1, sources * tok_dev)
        gate_slot = jnp.sum(jnp.where(onehot, gate, 0.0), axis=2)
        picks[q] = onehot.astype(BF16)
        tokens_x = got[:, :tok_dev].reshape(sources * tok_dev, part)
        tokens_g = got[:, tok_dev : 2 * tok_dev].reshape(sources * tok_dev, part)
        x = jnp.einsum("lst,td->lsd", picks[q], tokens_x, preferred_element_type=F32)
        g = jnp.einsum("lst,td->lsd", picks[q], tokens_g, preferred_element_type=F32)
        rows_x[q] = x.astype(BF16)
        rows_g[q] = (g * gate_slot[..., None]).astype(BF16)
        hidden = jnp.einsum("lrd,ldh->lrh", rows_x[q], pair_mats, preferred_element_type=F32)
        da = jnp.einsum("lrd,ldh->lrh", rows_g[q], down_mats, preferred_element_type=F32)
        sums = [hidden, da]
        for term in arrivals.pop(q, []):
            sums = [old + new.astype(F32) for old, new in zip(sums, term)]
        sent = [one.astype(BF16) for one in sums]
        if q:
            arrivals.setdefault(q & (q - 1), []).append([swap(one, q & -q) for one in sent])

    hidden, da = sums
    hg, hu = hidden[..., :ffn], hidden[..., ffn:]
    sig = jax.nn.sigmoid(hg)
    act = (hg * sig * hu).astype(BF16)
    dhu = (da * hg * sig).astype(BF16)
    dhg = (da * hu * sig * (1.0 + hg * (1.0 - sig))).astype(BF16)
    d_pair, acts = {0: jnp.concatenate([dhg, dhu], axis=2)}, {0: act}
    for held in (d_pair, acts):
        bit = replicas // 2
        while bit:
            for q in list(held):
                held[q ^ bit] = swap(held[q], bit)
            bit //= 2

    def stacked(pieces):
        return jnp.stack([pieces[q] for q in range(replicas)])

    return stacked(rows_x), stacked(rows_g), stacked(d_pair), stacked(acts), picks


def per_device(inputs, out_grad, routes, gates, weights, moment_one, moment_two):
    replicas, sources = lax.axis_size("rep"), lax.axis_size("exp")
    tok_dev, top = routes.shape
    part, local, kinds, ffn = weights.shape
    pair = 2 * ffn
    slots = sources * CAP
    me = lax.axis_index("rep")

    def swap(array, bits):
        if bits == 0:
            return array
        return lax.ppermute(array, "rep", [(i, i ^ bits) for i in range(replicas)])

    terms, rest = [routes.astype(BF16).T], gates.T
    for _ in range(3):
        head = lax.reduce_precision(rest, 8, 7)
        terms.append(head.astype(BF16))
        rest = rest - head
    mats = weights.transpose(1, 0, 2, 3).reshape(local, part, kinds * ffn)
    pair_mats = mats[..., :pair]
    half = max(replicas // 2, 1)
    at_once = 2 * replicas * sources * tok_dev * part + 20 * local * slots * kinds * ffn
    if replicas == 4 and sources % 2 == 0 and at_once < 32 << 20:
        meta = jnp.concatenate(terms, axis=1)
        meta = jnp.pad(meta, ((0, -top % 16), (0, 0)))
        rows_x, rows_g, d_pair, acts, rank = forward(
            inputs, out_grad, meta, weights, replicas, sources, CAP
        )
        index = jnp.arange(slots, dtype=F32)[:, None]
        picks = [(rank[q][:, None, :] == index).astype(BF16) for q in range(replicas)]
    else:
        rows_x, rows_g, d_pair, acts, picks = by_collectives(
            inputs, out_grad, terms, mats, top, sources, half, swap
        )

    token_dx = {}
    for q in range(replicas):
        slot_dx = jnp.einsum(
            "lrh,ldh->lrd", d_pair[q], pair_mats, preferred_element_type=F32
        ).astype(BF16)
        dx = jnp.einsum("lst,lsd->td", picks[q], slot_dx, preferred_element_type=F32)
        token_dx[q] = dx.astype(BF16).reshape(sources, tok_dev, part)
    home = {}
    for start in range(0, replicas, half):
        block = jnp.concatenate([token_dx[q] for q in range(start, start + half)], axis=1)
        block = lax.psum_scatter(block, "exp", scatter_dimension=0, tiled=False)
        for place in range(half):
            one = block[place * tok_dev : (place + 1) * tok_dev]
            home[start + place] = swap(one, start + place)
    home = jnp.stack([home[q] for q in range(replicas)])
    input_grad = jnp.concatenate(
        [lax.dynamic_index_in_dim(home, me ^ q, 0, keepdims=False) for q in range(replicas)],
        axis=1,
    )

    first_moment, second_moment, new_weights = expert_update(
        rows_x, rows_g, d_pair, acts, weights, moment_one, moment_two
    )
    return (input_grad, first_moment, second_moment, new_weights)


def solution(mesh):
    tokens = P(("rep", "exp"), None)
    experts = P("rep", "exp", None, None)
    return jax.shard_map(
        per_device,
        mesh=mesh,
        in_specs=(tokens, tokens, tokens, tokens, experts, experts, experts),
        out_specs=(tokens, experts, experts, experts),
        check_vma=False,
    )
```

profile of v0, /device:TPU:1, one launch (start us, length us, event | category | flops | bytes accessed | tf_op | source)
XLA Modules:
  0.0 429.9 jit_solution(1147089197309708071)
XLA Ops:
  7.2 0.0 reduce-scatter.3.cloned.1.call-start
  7.2 0.7 convert_bitcast_fusion
  7.9 0.7 reduce-precision_convert_fusion.1
  8.6 13.2 %copy.11 = bf16[512,8,3,384]{0,3,2,1:T(8,128)(2,1)} copy(bf16[512,8,3,384]{3,1,2,0:T(8,128)(2,1)} %param.11) | data formatting | bytes 18874368 | tf_op args[4]
  21.8 0.6 fusion.66.meta
  22.4 191.8 %gather_forward.1 = (bf16[4,8,144,512]{3,2,1,0:T(8,128)(2,1)}, bf16[4,8,144,512]{3,2,1,0:T(8,128)(2,1)}, bf16[4,8,144,768]{3,2,1,0:T(8,128)(2,1)}, bf16[4,8,144,384]{3,2,1,0:T(8,128)(2,1)}, f32[4,8,1024]{2,1,0:T(8,128)}) custom-call(bf16[128,2048]{1,0:T(8,128)(2,1)} %x.3, bf16[128,2048]{1,0:T(8,128)(2,1)} %g.1, bf16[16,512]{1,0:T(8,128)(2,1)} %fusion.66.meta, ...), custom_call_target="tpu_custom_call" | custom-call | tf_op jit(solution)/shard_map/gather_forward/pallas_call | solution.py:537
  214.2 0.8 slice_bitcast_fusion.6
  215.1 5.8 %bitcast_convert_fusion.3 = bf16[1024,512]{1,0:T(8,128)(2,1)S(1)} fusion(f32[8,1024]{1,0:T(8,128)S(1)} %get-tuple-element.28, bf16[8,512,1152]{1,2,0:T(8,128)(2,1)} %bitcast.87, bf16[4,8,144,768]{3,2,1,0:T(8,128)(2,1)} %get-tuple-element.13.refs_2_), kind=kOutput, calls=%fused_computation.25 | convolution fusion | flops 2116222976 | bytes 9142272 | tf_op jit(solution)/shard_map/lst,lsd->td/dot_general | solution.py:708
  220.9 5.8 %bitcast_convert_fusion.2 = bf16[1024,512]{1,0:T(8,128)(2,1)S(1)} fusion(f32[8,1024]{1,0:T(8,128)S(1)} %get-tuple-element.31, bf16[8,512,1152]{1,2,0:T(8,128)(2,1)} %bitcast.88, bf16[4,8,144,768]{3,2,1,0:T(8,128)(2,1)} %get-tuple-element.13.refs_2_), kind=kOutput, calls=%fused_computation.24 | convolution fusion | flops 2116222976 | bytes 9142272 | tf_op jit(solution)/shard_map/lst,lsd->td/dot_general | solution.py:708
  226.7 1.6 pad_maximum_fusion
  228.3 0.0 reduce-scatter.3.cloned.1.call-update
  228.3 0.0 reduce-scatter.5.cloned.1.call-start
  228.3 5.8 %bitcast_convert_fusion = bf16[1024,512]{1,0:T(8,128)(2,1)S(1)} fusion(f32[8,1024]{1,0:T(8,128)S(1)} %get-tuple-element.29, bf16[8,512,1152]{1,2,0:T(8,128)(2,1)} %bitcast.89, bf16[4,8,144,768]{3,2,1,0:T(8,128)(2,1)} %get-tuple-element.13.refs_2_), kind=kOutput, calls=%fused_computation.22 | convolution fusion | flops 2116222976 | bytes 9142272 | tf_op jit(solution)/shard_map/lst,lsd->td/dot_general | solution.py:708
  234.2 6.0 %bitcast_convert_fusion.1 = bf16[1024,512]{1,0:T(8,128)(2,1)S(1)} fusion(f32[8,1024]{1,0:T(8,128)S(1)} %get-tuple-element.30, bf16[8,512,1152]{1,2,0:T(8,128)(2,1)} %bitcast.90, bf16[4,8,144,768]{3,2,1,0:T(8,128)(2,1)} %get-tuple-element.13.refs_2_), kind=kOutput, calls=%fused_computation.23 | convolution fusion | flops 2116222976 | bytes 9142272 | tf_op jit(solution)/shard_map/lst,lsd->td/dot_general | solution.py:708
  240.2 1.6 pad_maximum_fusion.1
  241.7 0.0 reduce-scatter.5.cloned.1.call-update
  241.8 53.6 %reduce-scatter.3.cloned.1.call-done = bf16[1,256,512]{2,1,0:T(8,128)(2,1)} async-done(((bf16[8,256,512]{2,1,0:T(8,128)(2,1)}), bf16[1,256,512]{2,1,0:T(8,128)(2,1)}) %reduce-scatter.3.cloned.1.call-update) | async-done | bytes 262160 | tf_op jit(solution)/shard_map/reduce_scatter | solution.py:713
  295.4 1.0 fusion.69
  296.3 2.4 collective-permute-start
  298.8 68.2 %reduce-scatter.5.cloned.1.call-done = bf16[1,256,512]{2,1,0:T(8,128)(2,1)} async-done(((bf16[8,256,512]{2,1,0:T(8,128)(2,1)}), bf16[1,256,512]{2,1,0:T(8,128)(2,1)}) %reduce-scatter.5.cloned.1.call-update) | async-done | bytes 262160 | tf_op jit(solution)/shard_map/reduce_scatter | solution.py:713
  367.0 1.0 slice_bitcast_fusion.1
  367.9 1.2 collective-permute-start.1
  369.2 2.9 collective-permute-start.2
  372.0 50.0 %expert_update.1 = (f32[512,3,8,384]{3,2,1,0:T(8,128)}, f32[512,3,8,384]{3,2,1,0:T(8,128)}, bf16[512,3,8,384]{3,2,1,0:T(8,128)(2,1)}) custom-call(bf16[4,8,144,512]{3,2,1,0:T(8,128)(2,1)} %get-tuple-element.14.refs_0_, bf16[4,8,144,512]{3,2,1,0:T(8,128)(2,1)} %get-tuple-element.15.refs_1_, bf16[4,8,144,768]{3,2,1,0:T(8,128)(2,1)} %get-tuple-element.13.refs_2_, ...), custom_call_target="tpu_custom_call" | custom-call | flops 5435817984 | bytes 94371840 | tf_op jit(solution)/shard_map/expert_update/pallas_call | solution.py:158
  422.0 0.0 collective-permute-done
  422.0 0.0 collective-permute-done.1
  422.0 0.0 collective-permute-done.2
  422.0 0.1 pad_maximum_fusion.2
  422.2 0.8 pad_maximum_fusion.3
  (1 shorter events, 0.0 us)
Async XLA Ops:
  7.2 288.2 %reduce-scatter.3.cloned.1.call-start = ((), (), s32[]{:S(2)}) async-start(), calls=%async_computation.2 | async-start | bytes 2359296 | tf_op jit(solution)/shard_map/reduce_scatter | solution.py:713
  228.3 138.7 %reduce-scatter.5.cloned.1.call-start = ((), (), s32[]{:S(2)}) async-start(), calls=%async_computation.3 | async-start | bytes 2359296 | tf_op jit(solution)/shard_map/reduce_scatter | solution.py:713
  296.3 125.7 %collective-permute-start = (bf16[128,512]{1,0:T(8,128)(2,1)S(1)}, bf16[128,512]{1,0:T(8,128)(2,1)S(1)}, u32[]{:S(2)}, u32[]{:S(2)}) collective-permute-start(bf16[128,512]{1,0:T(8,128)(2,1)S(1)} %get-tuple-element.25), channel_id=1, source_target_pairs={{0,8},{8,0},{16,24},{24,16},{1,9},{9,1},{17,25},{25,17},{2,10},{10... | collective-permute-start | bytes 393224 | tf_op jit(solution)/shard_map/ppermute | solution.py:679
  367.9 54.1 %collective-permute-start.1 = (bf16[128,512]{1,0:T(8,128)(2,1)S(1)}, bf16[128,512]{1,0:T(8,128)(2,1)S(1)}, u32[]{:S(2)}, u32[]{:S(2)}) collective-permute-start(bf16[128,512]{1,0:T(8,128)(2,1)S(1)} %get-tuple-element.26), channel_id=1, source_target_pairs={{0,16},{8,24},{16,0},{24,8},{1,17},{9,25},{17,1},{25,9},{2,18},{10... | collective-permute-start | bytes 393224 | tf_op jit(solution)/shard_map/ppermute | solution.py:679
  369.2 52.9 %collective-permute-start.2 = (bf16[128,512]{1,0:T(8,128)(2,1)S(1)}, bf16[128,512]{1,0:T(8,128)(2,1)S(1)}, u32[]{:S(2)}, u32[]{:S(2)}) collective-permute-start(bf16[128,512]{1,0:T(8,128)(2,1)S(1)} %get-tuple-element.27), channel_id=1, source_target_pairs={{0,24},{8,16},{16,8},{24,0},{1,25},{9,17},{17,9},{25,1},{2,26},{10... | collective-permute-start | bytes 393224 | tf_op jit(solution)/shard_map/ppermute | solution.py:679
Sparse Core Ops, SparseCore 0:
  228.4 66.9 reduce-scatter.2
  299.5 67.4 reduce-scatter.4
where the time goes:
time: 431 us; the launch traced here: 430 us
  Pallas kernels  242 us (56%)
  waiting for transfers between devices  122 us (28%)
  matrix products  23.5 us (5%)
  local copies, waits for them, and re-layouts  16.1 us (4%)
  between operations  14.2 us (3%)
  starting transfers between devices  6.6 us (2%)
  other arithmetic  6.01 us (1%)
    pallas_call x1, Pallas kernels, forward(): pl.pallas_call(functools.partial(forward_kernel, dims), out_shape=(jax.Sh...  192 us
    reduce_scatter x2, waiting for transfers between devices, per_device(): block = lax.psum_scatter(block, 'exp', scatter_dimension=0, tiled=False)  122 us
    pallas_call x1, Pallas kernels, expert_update(): pl.pallas_call(kernel, out_shape=tuple((jax.ShapeDtypeStruct(a.shape, a.d...  50 us
    dot_general x4, matrix products, per_device(): jnp.einsum('lst,lsd->td', picks[q], slot_dx, preferred_element_type=F32)  23.5 us
    unnamed x1, local copies, waits for them, and re-layouts  13.2 us
  transfers between devices with their start and end apart: 5, of which 2 were waited for; matrix products, arithmetic and copies ran while one was open for 4% of the time, Pallas kernels for 12%

commit v1 on v0

--- a/solution.py
+++ b/solution.py
@@ -22,8 +22,140 @@
 BF16 = jnp.bfloat16
 
 
+MESH = pl.DeviceIdType.MESH
+
+
+def flip(index, bits):
+    for bit in (1, 2):
+        if bits & bit:
+            index = index + bit * (1 - 2 * ((index // bit) % 2))
+    return index
+
+
+class Scatter:
+    def __init__(self, parts, sources, mine, theirs, refs):
+        self.parts, self.mine, self.theirs = parts, mine, theirs
+        self.from_side, self.from_z, self.total, self.home = refs[:4]
+        self.y_send, self.y_got, self.z_send, self.z_got, self.h_send, self.h_got = refs[4:]
+        self.me, self.ex = lax.axis_index("rep"), lax.axis_index("exp")
+        self.col, self.z, self.line = self.ex % 2, self.ex // 2, sources // 2
+        self.side = self.ex + 1 - 2 * self.col
+        self.above, self.below = self.z + 1 < self.line, self.z >= 1
+
+    def across(self, j, level):
+        return pltpu.make_async_remote_copy(
+            src_ref=self.theirs(j, level),
+            dst_ref=self.from_side.at[j, level],
+            send_sem=self.y_send.at[j, level],
+            recv_sem=self.y_got.at[j, level],
+            device_id={"exp": self.side},
+            device_id_type=MESH,
+        )
+
+    def along(self, j, level, way):
+        return pltpu.make_async_remote_copy(
+            src_ref=self.mine(j, level),
+            dst_ref=self.from_z.at[way, j, level],
+            send_sem=self.z_send.at[way, j, level],
+            recv_sem=self.z_got.at[way, j, level],
+            device_id={"exp": self.ex + (2 if way == 0 else -2)},
+            device_id_type=MESH,
+        )
+
+    def homeward(self, j):
+        q = self.parts[j]
+        if q == 0:
+            return pltpu.make_async_copy(self.total.at[j], self.home.at[j], self.h_got.at[j])
+        return pltpu.make_async_remote_copy(
+            src_ref=self.total.at[j],
+            dst_ref=self.home.at[j],
+            send_sem=self.h_send.at[j],
+            recv_sem=self.h_got.at[j],
+            device_id={"rep": flip(self.me, q)},
+            device_id_type=MESH,
+        )
+
+    def begin(self, j):
+        for level in range(self.line):
+            self.across(j, level).start()
+
+    def add(self, j, level, ways, into):
+        into[...] = sum(
+            [self.from_z[way, j, level].astype(F32) for way in ways],
+            self.mine(j, level)[...].astype(F32) + self.from_side[j, level].astype(F32),
+        ).astype(BF16)
+
+    def step(self, j, t):
+        for way, level, near, fed in (
+            (0, self.line - 1 - t, self.z < self.line - 1 - t, self.below),
+            (1, t, self.z > t, self.above),
+        ):
+
+            @pl.when(near)
+            def _():
+                self.across(j, level).wait_recv()
+
+                @pl.when(fed)
+                def _():
+                    self.along(j, level, way).wait_recv()
+                    self.add(j, level, (way,), self.mine(j, level))
+
+                @pl.when(jnp.logical_not(fed))
+                def _():
+                    self.add(j, level, (), self.mine(j, level))
+
+                self.along(j, level, way).start()
+
+    def finish(self, j):
+        for level in range(self.line):
+
+            @pl.when(self.z == level)
+            def _():
+                self.across(j, level).wait_recv()
+                ways = [0] * (level >= 1) + [1] * (level + 1 < self.line)
+                for way in ways:
+                    self.along(j, level, way).wait_recv()
+                self.add(j, level, ways, self.total.at[j])
+
+        self.homeward(j).start()
+
+    def end(self, j):
+        if self.parts[j]:
+            self.homeward(j).wait_recv()
+            self.homeward(j).wait_send()
+        else:
+            self.homeward(j).wait()
+        for level in range(self.line):
+            self.across(j, level).wait_send()
+
+            @pl.when(self.z < level)
+            def _():
+                self.along(j, level, 0).wait_send()
+
+            @pl.when(self.z > level)
+            def _():
+                self.along(j, level, 1).wait_send()
+
+
+def scatter_scratch(parts, sources, tok, part):
+    line = sources // 2
+    dma = pltpu.SemaphoreType.DMA
+    return [
+        pltpu.VMEM((parts, line, tok, part), BF16),
+        pltpu.VMEM((2, parts, line, tok, part), BF16),
+        pltpu.VMEM((parts, tok, part), BF16),
+        pltpu.VMEM((parts, tok, part), BF16),
+        dma((parts, line)),
+        dma((parts, line)),
+        dma((2, parts, line)),
+        dma((2, parts, line)),
+        dma((parts,)),
+        dma((parts,)),
+    ]
+
+
 def update_kernel(dims, *refs):
-    (replicas, slots, part, local, kinds, ffn, block, depth, _) = dims
+    (replicas, slots, part, local, kinds, ffn, block, depth) = dims
     pieces, refs = refs[:4], refs[4:]
     m_one, m_two, w_in, o_one, o_two, w_out = refs[:6]
     bufs, (grad, b_one, b_two, b_w, in_sem, load_sem, store_sem) = refs[6:10], refs[10:]
@@ -96,8 +228,7 @@
     correct_one = 1.0 - beta_one**step_count
     correct_two = 1.0 - beta_two**step_count
 
-    @pl.loop(0, blocks)
-    def _(i):
+    def advance(i):
         s = lax.rem(i, depth)
         for copy in moves(i, False):
             copy.wait()
@@ -136,6 +267,8 @@
             for copy in moves(i - 1 + depth, False):
                 copy.start()
 
+    pl.loop(0, blocks)(advance)
+
     @pl.loop(max(blocks - depth, 0), blocks)
     def _(i):
         for copy in moves(i, True):
@@ -152,14 +285,15 @@
     held = [a.transpose(0, 2, 1, 3) for a in (moment_one, moment_two, weights)]
     depth = 10
     any_spec = pl.BlockSpec(memory_space=pl.ANY)
+    out_shape = tuple(jax.ShapeDtypeStruct(a.shape, a.dtype) for a in held)
     kernel = functools.partial(
-        update_kernel, (replicas, slots, part, local, kinds, ffn, block, depth, None)
+        update_kernel, (replicas, slots, part, local, kinds, ffn, block, depth)
     )
     outs = pl.pallas_call(
         kernel,
-        out_shape=tuple(jax.ShapeDtypeStruct(a.shape, a.dtype) for a in held),
+        out_shape=out_shape,
         in_specs=[any_spec] * (len(pieces) + 3),
-        out_specs=(any_spec,) * 3,
+        out_specs=(any_spec,) * len(out_shape),
         scratch_shapes=[
             pltpu.VMEM((twin, rows, part), BF16),
             pltpu.VMEM((twin, rows, part), BF16),
@@ -184,20 +318,13 @@
     return [a.transpose(0, 2, 1, 3) for a in outs]
 
 
-MESH = pl.DeviceIdType.MESH
-
-
-def flip(index, bits):
-    for bit in (1, 2):
-        if bits & bit:
-            index = index + bit * (1 - 2 * ((index // bit) % 2))
-    return index
-
-
-def forward_kernel(dims, x, g, meta, weights, out_x, out_g, out_pair, out_act, out_rank, *scratch):
+def forward_kernel(dims, x, g, meta, weights, out_x, out_g, out_pair, out_act, out_dx, out_home, *scratch):
     replicas, sources, tok, part, local, slots, ffn, cap = dims
     (gx, gg, gm, w, rank, gate, rows_x, rows_g, outgoing, incoming, own, held, raw, turned) = scratch[:14]
-    (own_send, got, sent, w_sem, part_send, part_got, d_send, d_got, out_sem) = scratch[14:]
+    sum_dx, scratch = scratch[14], scratch[15:]
+    (own_send, got, sent, w_sem, part_send, part_got, d_send, d_got, out_sem, row_sem) = scratch[:10]
+    scatter_refs = scratch[10:]
+    ring = rows_x.shape[0]
     me, ex = lax.axis_index("rep"), lax.axis_index("exp")
     col, z = ex % 2, ex // 2
     line = sources // 2
@@ -364,9 +491,10 @@
         )
 
     def row_out(l, q):
+        slot = (l + (replicas - 1 - q) * local) % ring
         return (
-            pltpu.make_async_copy(rows_x.at[q, l], out_x.at[q, l], out_sem.at[0, q, l]),
-            pltpu.make_async_copy(rows_g.at[q, l], out_g.at[q, l], out_sem.at[1, q, l]),
+            pltpu.make_async_copy(rows_x.at[slot], out_x.at[q, l], row_sem.at[0, slot]),
+            pltpu.make_async_copy(rows_g.at[slot], out_g.at[q, l], row_sem.at[1, slot]),
         )
 
     def piece(l, q):
@@ -379,8 +507,16 @@
         tokens_g = gg[q].reshape(sources * tok, part)
         rx = jnp.dot(pick, tokens_x, preferred_element_type=F32).astype(BF16)
         rg = (jnp.dot(pick, tokens_g, preferred_element_type=F32) * gates).astype(BF16)
-        rows_x[q, l] = rx
-        rows_g[q, l] = rg
+        turn_of = l + (replicas - 1 - q) * local
+        slot = turn_of % ring
+
+        @pl.when(turn_of >= ring)
+        def _():
+            for copy in row_out(l, q):
+                copy.wait()
+
+        rows_x[slot] = rx
+        rows_g[slot] = rg
         for copy in row_out(l, q):
             copy.start()
         hidden = jnp.dot(rx, w[l, :, :pair], preferred_element_type=F32)
@@ -418,10 +554,10 @@
     def d_out(l, q):
         return (
             pltpu.make_async_copy(
-                held.at[q, l, :, pl.ds(0, pair)], out_pair.at[q, l], out_sem.at[2, q, l]
+                held.at[q, l, :, pl.ds(0, pair)], out_pair.at[q, l], out_sem.at[0, q, l]
             ),
             pltpu.make_async_copy(
-                held.at[q, l, :, pl.ds(pair, ffn)], out_act.at[q, l], out_sem.at[3, q, l]
+                held.at[q, l, :, pl.ds(pair, ffn)], out_act.at[q, l], out_sem.at[1, q, l]
             ),
         )
 
@@ -470,30 +606,97 @@
         settle(q)
         prepare(q)
 
-    @pl.loop(0, local + 2)
+    @pl.loop(0, local)
     def _(l):
-        @pl.when(l < local)
-        def _():
-            piece(l, order[-1])
-            finish(l)
-
-        @pl.when(l >= 2)
-        def _():
-            pass_on(l - 2)
-
-    rank_copy = pltpu.make_async_copy(rank, out_rank, w_sem.at[0])
-    rank_copy.start()
+        piece(l, order[-1])
+        finish(l)
+
+    def sent_blocks(q, n):
+        @pl.loop(0, line)
+        def _(level):
+            slot = 2 * level + col
+            hop(q, n, slot, 0).wait_send()
+
+            @pl.when(above & (level <= z))
+            def _():
+                hop(q, n, slot, 1).wait_send()
+
+            @pl.when(below & (level >= z))
+            def _():
+                hop(q, n, slot, 2).wait_send()
+
+    def add_dx(l, q, total):
+        hit = lax.broadcasted_iota(jnp.int32, (slots, sources * tok), 0).astype(F32)
+        pick = jnp.where(hit == rank[q, pl.ds(l, 1), :], 1.0, 0.0).astype(BF16)
+        slot_dx = lax.dot_general(
+            held[q, l, :, :pair],
+            w[l, :, :pair],
+            (((1,), (1,)), ((), ())),
+            preferred_element_type=F32,
+        ).astype(BF16)
+        sum_dx[total] += lax.dot_general(
+            pick, slot_dx, (((0,), (0,)), ((), ())), preferred_element_type=F32
+        )
+
+    def round_dx(q, total):
+        sent_blocks(q, 1)
+        gx[q] = sum_dx[total].reshape(sources, tok, part).astype(BF16)
+
+    near = Scatter(
+        (0, 1),
+        sources,
+        lambda j, level: gx.at[j, 2 * level + col],
+        lambda j, level: gx.at[j, 2 * level + 1 - col],
+        scatter_refs,
+    )
+    sum_dx[...] = jnp.zeros_like(sum_dx)
+
+    @pl.loop(0, local)
+    def _(l):
+        add_dx(l, 0, 0)
+
+    round_dx(0, 0)
+    near.begin(0)
 
     @pl.loop(0, local)
     def _(l):
         grads_to(l, 0).wait_recv()
         for copy in d_out(l, 1):
             copy.start()
-        grads_to(l, 2).wait_recv()
-        for copy in d_out(l, 3):
-            copy.start()
-
-    rank_copy.wait()
+        add_dx(l, 1, 1)
+
+    round_dx(1, 1)
+    near.begin(1)
+    sum_dx[...] = jnp.zeros_like(sum_dx)
+    for t in range(line - 1):
+        for j in range(2):
+            near.step(j, t)
+    for j in range(2):
+        near.finish(j)
+
+    @pl.loop(0, local + 1)
+    def _(l):
+        @pl.when(l < local)
+        def _():
+            pass_on(l)
+            add_dx(l, 2, 0)
+
+        @pl.when(l >= 1)
+        def _():
+            grads_to(l - 1, 2).wait_recv()
+            for copy in d_out(l - 1, 3):
+                copy.start()
+            add_dx(l - 1, 3, 1)
+
+    last = []
+    for q in (2, 3):
+        round_dx(q, q - 2)
+        last.append(pltpu.make_async_copy(gx.at[q], out_dx.at[:, q - 2], w_sem.at[q - 2]))
+        last[-1].start()
+    for j in range(2):
+        near.end(j)
+    home_copy = pltpu.make_async_copy(near.home, out_home, own_send.at[0, 0])
+    home_copy.start()
 
     @pl.loop(0, local)
     def _(l):
@@ -502,33 +705,30 @@
         for way in range(3):
             grads_to(l, way).wait_send()
         for q in range(replicas):
-            for copy in row_out(l, q) + d_out(l, q):
+            for copy in d_out(l, q):
+                copy.wait()
+
+        @pl.when(l >= local - ring)
+        def _():
+            for copy in row_out(l, 0):
                 copy.wait()
 
     for q in order:
         for n in range(3):
             if q:
                 first(q, n).wait_send()
-
-            @pl.loop(0, line)
-            def _(level):
-                slot = 2 * level + col
-                hop(q, n, slot, 0).wait_send()
-
-                @pl.when(above & (level <= z))
-                def _():
-                    hop(q, n, slot, 1).wait_send()
-
-                @pl.when(below & (level >= z))
-                def _():
-                    hop(q, n, slot, 2).wait_send()
+            if n != 1:
+                sent_blocks(q, n)
+    for copy in (*last, home_copy):
+        copy.wait()
 
 
 def forward(inputs, out_grad, meta, weights, replicas, sources, cap):
     tok = inputs.shape[0]
     part, local, kinds, ffn = weights.shape
     width = kinds * ffn
-    chunk = part // 8
+    chunk = part // 16
+    ring = min(4, local)
     slots = sources * cap
     dims = (replicas, sources, tok, part, local, slots, ffn, cap)
     any_spec = pl.BlockSpec(memory_space=pl.ANY)
@@ -541,10 +741,11 @@
             jax.ShapeDtypeStruct((*rows, part), BF16),
             jax.ShapeDtypeStruct((*rows, 2 * ffn), BF16),
             jax.ShapeDtypeStruct((*rows, ffn), BF16),
-            jax.ShapeDtypeStruct((replicas, local, sources * tok), F32),
+            jax.ShapeDtypeStruct((sources, 2, tok, part), BF16),
+            jax.ShapeDtypeStruct((2, tok, part), BF16),
         ),
         in_specs=[any_spec] * 4,
-        out_specs=(any_spec,) * 5,
+        out_specs=(any_spec,) * 6,
         scratch_shapes=[
             pltpu.VMEM((replicas, sources, tok, part), BF16),
             pltpu.VMEM((replicas, sources, tok, part), BF16),
@@ -552,14 +753,15 @@
             pltpu.VMEM((local, part, width), BF16),
             pltpu.VMEM((replicas, local, sources * tok), F32),
             pltpu.VMEM((local, sources * tok), F32),
-            pltpu.VMEM((*rows, part), BF16),
-            pltpu.VMEM((*rows, part), BF16),
+            pltpu.VMEM((ring, slots, part), BF16),
+            pltpu.VMEM((ring, slots, part), BF16),
             pltpu.VMEM((2, local, slots, width), BF16),
             pltpu.VMEM((3, local, slots, width), BF16),
             pltpu.VMEM((local, slots, width), F32),
             pltpu.VMEM((*rows, width), BF16),
             pltpu.VMEM((2, chunk, kinds, local, ffn), BF16),
             pltpu.VMEM((width // 128, local * chunk, 128), F32),
+            pltpu.VMEM((2, sources * tok, part), F32),
             dma((replicas, 3)),
             dma((replicas, 3, sources)),
             dma((3, replicas, 3, sources)),
@@ -568,7 +770,9 @@
             dma((3, local)),
             dma((3, local)),
             dma((3, local)),
-            dma((4, replicas, local)),
+            dma((2, replicas, local)),
+            dma((2, ring)),
+            *scatter_scratch(2, sources, tok, part),
         ],
         compiler_params=pltpu.CompilerParams(
             collective_id=0, has_side_effects=True, vmem_limit_bytes=63 << 20
@@ -577,14 +781,15 @@
     )(inputs, out_grad, meta, weights.transpose(0, 2, 1, 3))
 
 
-def by_collectives(inputs, out_grad, terms, mats, top, sources, half, swap):
+def by_collectives(inputs, out_grad, terms, weights, top, sources, swap):
     replicas = lax.axis_size("rep")
     me = lax.axis_index("rep")
     tok_dev = inputs.shape[0]
-    local, part, width = mats.shape
-    ffn = width // 3
+    part, local, kinds, ffn = weights.shape
     pair = 2 * ffn
     slots = sources * CAP
+    half = max(replicas // 2, 1)
+    mats = weights.transpose(1, 0, 2, 3).reshape(local, part, kinds * ffn)
     meta = jnp.concatenate(terms).reshape(-1, part)
     meta_rows = meta.shape[0]
     pad = -meta_rows % 16
@@ -659,47 +864,6 @@
                 held[q ^ bit] = swap(held[q], bit)
             bit //= 2
 
-    def stacked(pieces):
-        return jnp.stack([pieces[q] for q in range(replicas)])
-
-    return stacked(rows_x), stacked(rows_g), stacked(d_pair), stacked(acts), picks
-
-
-def per_device(inputs, out_grad, routes, gates, weights, moment_one, moment_two):
-    replicas, sources = lax.axis_size("rep"), lax.axis_size("exp")
-    tok_dev, top = routes.shape
-    part, local, kinds, ffn = weights.shape
-    pair = 2 * ffn
-    slots = sources * CAP
-    me = lax.axis_index("rep")
-
-    def swap(array, bits):
-        if bits == 0:
-            return array
-        return lax.ppermute(array, "rep", [(i, i ^ bits) for i in range(replicas)])
-
-    terms, rest = [routes.astype(BF16).T], gates.T
-    for _ in range(3):
-        head = lax.reduce_precision(rest, 8, 7)
-        terms.append(head.astype(BF16))
-        rest = rest - head
-    mats = weights.transpose(1, 0, 2, 3).reshape(local, part, kinds * ffn)
-    pair_mats = mats[..., :pair]
-    half = max(replicas // 2, 1)
-    at_once = 2 * replicas * sources * tok_dev * part + 20 * local * slots * kinds * ffn
-    if replicas == 4 and sources % 2 == 0 and at_once < 32 << 20:
-        meta = jnp.concatenate(terms, axis=1)
-        meta = jnp.pad(meta, ((0, -top % 16), (0, 0)))
-        rows_x, rows_g, d_pair, acts, rank = forward(
-            inputs, out_grad, meta, weights, replicas, sources, CAP
-        )
-        index = jnp.arange(slots, dtype=F32)[:, None]
-        picks = [(rank[q][:, None, :] == index).astype(BF16) for q in range(replicas)]
-    else:
-        rows_x, rows_g, d_pair, acts, picks = by_collectives(
-            inputs, out_grad, terms, mats, top, sources, half, swap
-        )
-
     token_dx = {}
     for q in range(replicas):
         slot_dx = jnp.einsum(
@@ -715,13 +879,51 @@
             one = block[place * tok_dev : (place + 1) * tok_dev]
             home[start + place] = swap(one, start + place)
     home = jnp.stack([home[q] for q in range(replicas)])
+
+    def stacked(pieces):
+        return jnp.stack([pieces[q] for q in range(replicas)])
+
+    return stacked(rows_x), stacked(rows_g), stacked(d_pair), stacked(acts), home
+
+
+def per_device(inputs, out_grad, routes, gates, weights, moment_one, moment_two):
+    replicas, sources = lax.axis_size("rep"), lax.axis_size("exp")
+    tok_dev, top = routes.shape
+    part, local, kinds, ffn = weights.shape
+    slots = sources * CAP
+    me = lax.axis_index("rep")
+
+    def swap(array, bits):
+        if bits == 0:
+            return array
+        return lax.ppermute(array, "rep", [(i, i ^ bits) for i in range(replicas)])
+
+    terms, rest = [routes.astype(BF16).T], gates.T
+    for _ in range(3):
+        head = lax.reduce_precision(rest, 8, 7)
+        terms.append(head.astype(BF16))
+        rest = rest - head
+    at_once = 2 * replicas * sources * tok_dev * part + 20 * local * slots * kinds * ffn
+    if replicas == 4 and sources % 2 == 0 and at_once < 32 << 20:
+        meta = jnp.concatenate(terms, axis=1)
+        meta = jnp.pad(meta, ((0, -top % 16), (0, 0)))
+        *grown, dx, near = forward(inputs, out_grad, meta, weights, replicas, sources, CAP)
+        far = lax.psum_scatter(
+            dx.reshape(sources, 2 * tok_dev, part), "exp", scatter_dimension=0, tiled=False
+        )
+        far = [swap(far[j * tok_dev : (j + 1) * tok_dev], j + 2) for j in range(2)]
+        first_moment, second_moment, new_weights = expert_update(
+            *grown, weights, moment_one, moment_two
+        )
+        home = jnp.concatenate([near, jnp.stack(far)])
+    else:
+        *grown, home = by_collectives(inputs, out_grad, terms, weights, top, sources, swap)
+        first_moment, second_moment, new_weights = expert_update(
+            *grown, weights, moment_one, moment_two
+        )
     input_grad = jnp.concatenate(
         [lax.dynamic_index_in_dim(home, me ^ q, 0, keepdims=False) for q in range(replicas)],
         axis=1,
-    )
-
-    first_moment, second_moment, new_weights = expert_update(
-        rows_x, rows_g, d_pair, acts, weights, moment_one, moment_two
     )
     return (input_grad, first_moment, second_moment, new_weights)
 

time: 431 us -> 336 us (0.78)
  waiting for transfers between devices: 122 us -> 65.5 us
  matrix products: 23.5 us -> 0 us
  local copies, waits for them, and re-layouts: 16.1 us -> 1.03 us
  Pallas kernels: 242 us -> 248 us
    reduce_scatter x2 -> x1, waiting for transfers between devices: 122 us -> 65.5 us  [per_device(): lax.psum_scatter(dx.reshape(sources, 2 * tok_dev, part), 'exp', scatter_d...]
    dot_general x4 -> x0, matrix products: 23.5 us -> none  [per_device(): jnp.einsum('lst,lsd->td', picks[q], slot_dx, preferred_element_type=F32)]
    unnamed x1 -> x2, local copies, waits for them, and re-layouts: 13.2 us -> 0.01 us
    pallas_call x1, Pallas kernels: 192 us -> 199 us  [forward(): pl.pallas_call(functools.partial(forward_kernel, dims), out_shape=(jax.Sh...]
  transfers between devices with their start and end apart: 5 -> 3, of which waited for: 2 -> 1; matrix products, arithmetic and copies ran while one was open for 4% -> 0% of each run, Pallas kernels for 12% -> 15%
where the time goes in v1:
time: 336 us
  Pallas kernels  248 us (74%)
  waiting for transfers between devices  65.5 us (19%)
  between operations  14.1 us (4%)
  starting transfers between devices  3.94 us (1%)
    pallas_call x1, Pallas kernels, forward(): pl.pallas_call(functools.partial(forward_kernel, dims), out_shape=(jax.Sh...  199 us
    reduce_scatter x1, waiting for transfers between devices, per_device(): lax.psum_scatter(dx.reshape(sources, 2 * tok_dev, part), 'exp', scatter_d...  65.5 us
    pallas_call x1, Pallas kernels, expert_update(): pl.pallas_call(kernel, out_shape=out_shape, in_specs=[any_spec] * (len(pi...  49.9 us
  transfers between devices with their start and end apart: 3, of which 1 were waited for; matrix products, arithmetic and copies ran while one was open for 0% of the time, Pallas kernels for 15%

profile of v1, /device:TPU:1, one launch (start us, length us, event | category | flops | bytes accessed | tf_op | source)
XLA Modules:
  0.0 336.0 jit_solution(10510282605734791533)
XLA Ops:
  7.2 0.0 reduce-scatter.2.cloned.1.call-start
  7.2 0.7 convert_bitcast_fusion
  7.9 0.7 reduce-precision_convert_fusion.1
  8.6 0.6 fusion.6.meta
  9.2 198.5 %gather_forward.1 = (bf16[4,8,144,512]{3,2,1,0:T(8,128)(2,1)}, bf16[4,8,144,512]{3,2,1,0:T(8,128)(2,1)}, bf16[4,8,144,768]{3,2,1,0:T(8,128)(2,1)}, bf16[4,8,144,...) custom-call(bf16[128,2048]{1,0:T(8,128)(2,1)} %x.3, bf16[128,2048]{1,0:T(8,128)(2,1)} %g.1, ...), custom_call_target="tpu_custom_call" | custom-call | tf_op jit(solution)/shard_map/gather_forward/pallas_call | solution.py:737
  207.8 0.0 reduce-scatter.2.cloned.1.call-update
  207.8 65.5 %reduce-scatter.2.cloned.1.call-done = bf16[1,256,512]{2,1,0:T(8,128)(2,1)} async-done(((bf16[8,256,512]{2,1,0:T(8,128)(2,1)}), bf16[1,256,512]{2,1,0:T(8,128)(2,1)}) %reduce-scatter.2.cloned.1.call-update) | async-done | bytes 262160 | tf_op jit(solution)/shard_map/reduce_scatter | solution.py:911
  273.3 1.0 slice_bitcast_fusion.1
  274.3 1.3 collective-permute-start
  275.5 2.6 collective-permute-start.1
  278.2 0.0 copy-start
  278.2 49.9 %expert_update.1 = (f32[512,3,8,384]{3,2,1,0:T(8,128)}, f32[512,3,8,384]{3,2,1,0:T(8,128)}, bf16[512,3,8,384]{3,2,1,0:T(8,128)(2,1)}) custom-call(bf16[4,8,144,512]{3,2,1,0:T(8,128)(2,1)} %get-tuple-element.15.refs_0_, bf16[4,8,144,512]{3,2,1,0:T(8,128)(2,1)} %get-tuple-element.16.refs_1_, bf16[4,8,144,768]{3,2,1,0:T(8,128)(2,1)} %get-tuple-element.17.refs_2_, ...), custom_call_target="tpu_custom_call" | custom-call | flops 5435817984 | bytes 94371840 | tf_op jit(solution)/shard_map/expert_update/pallas_call | solution.py:292
  328.1 0.0 collective-permute-done
  328.1 0.0 collective-permute-done.1
  328.2 0.0 copy-done
  328.2 0.1 pad_maximum_fusion
  328.3 0.8 pad_maximum_fusion.1
  (1 shorter events, 0.0 us)
Async XLA Ops:
  7.2 266.1 %reduce-scatter.2.cloned.1.call-start = ((), (), s32[]{:S(2)}) async-start(), calls=%async_computation.1 | async-start | bytes 2359296 | tf_op jit(solution)/shard_map/reduce_scatter | solution.py:911
  274.3 53.9 %collective-permute-start = (bf16[128,512]{1,0:T(8,128)(2,1)S(1)}, bf16[128,512]{1,0:T(8,128)(2,1)S(1)}, u32[]{:S(2)}, u32[]{:S(2)}) collective-permute-start(bf16[128,512]{1,0:T(8,128)(2,1)S(1)} %get-tuple-element.26), channel_id=1, source_target_pairs={{0,16},{8,24},{16,0},{24,8},{1,17},{9,25},{17,1},{25,9},{2,18},{10... | collective-permute-start | bytes 393224 | tf_op jit(solution)/shard_map/ppermute | solution.py:899
  275.5 52.6 %collective-permute-start.1 = (bf16[128,512]{1,0:T(8,128)(2,1)S(1)}, bf16[128,512]{1,0:T(8,128)(2,1)S(1)}, u32[]{:S(2)}, u32[]{:S(2)}) collective-permute-start(bf16[128,512]{1,0:T(8,128)(2,1)S(1)} %get-tuple-element.27), channel_id=1, source_target_pairs={{0,24},{8,16},{16,8},{24,0},{1,25},{9,17},{17,9},{25,1},{2,26},{10... | collective-permute-start | bytes 393224 | tf_op jit(solution)/shard_map/ppermute | solution.py:899
  278.2 50.0 %copy-start = (bf16[2,128,512]{2,1,0:T(8,128)(2,1)S(1)}, bf16[2,128,512]{2,1,0:T(8,128)(2,1)}, u32[]{:S(2)}) copy-start(bf16[2,128,512]{2,1,0:T(8,128)(2,1)} %get-tuple-element.13) | copy-start | bytes 786436
Sparse Core Ops, SparseCore 0:
  207.9 65.3 reduce-scatter.1

commit v2 on v1

--- a/solution.py
+++ b/solution.py
@@ -26,7 +26,8 @@
 
 
 def flip(index, bits):
-    for bit in (1, 2):
+    for place in range(bits.bit_length()):
+        bit = 1 << place
         if bits & bit:
             index = index + bit * (1 - 2 * ((index // bit) % 2))
     return index
@@ -76,8 +77,9 @@
         )
 
     def begin(self, j):
-        for level in range(self.line):
-            self.across(j, level).start()
+        for t in range((self.line + 1) // 2):
+            for level in sorted({self.line - 1 - t, t}, reverse=True):
+                self.across(j, level).start()
 
     def add(self, j, level, ways, into):
         into[...] = sum(
@@ -318,12 +320,13 @@
     return [a.transpose(0, 2, 1, 3) for a in outs]
 
 
-def forward_kernel(dims, x, g, meta, weights, out_x, out_g, out_pair, out_act, out_dx, out_home, *scratch):
+def forward_kernel(dims, x, g, meta, weights, out_x, out_g, out_pair, out_act, out_home, *scratch):
     replicas, sources, tok, part, local, slots, ffn, cap = dims
+    out_dx, scratch = scratch[:sources], scratch[sources:]
     (gx, gg, gm, w, rank, gate, rows_x, rows_g, outgoing, incoming, own, held, raw, turned) = scratch[:14]
     sum_dx, scratch = scratch[14], scratch[15:]
     (own_send, got, sent, w_sem, part_send, part_got, d_send, d_got, out_sem, row_sem) = scratch[:10]
-    scatter_refs = scratch[10:]
+    far_sem, scatter_refs = scratch[10], scratch[11:]
     ring = rows_x.shape[0]
     me, ex = lax.axis_index("rep"), lax.axis_index("exp")
     col, z = ex % 2, ex // 2
@@ -412,8 +415,43 @@
         for n in range(3):
             first(q, n).start()
 
-    def relay(q, step):
-        for n in range(3):
+    def onward(q, n, slot, ways):
+        for way in ways:
+
+            @pl.when(above if way == 1 else below)
+            def _():
+                hop(q, n, slot, way).start()
+
+    def relay_both(q, n, step):
+        if step == 0:
+            (first(q, n).wait_recv if q else first(q, n).wait)()
+            hop(q, n, ex, 0).start()
+            onward(q, n, ex, (1, 2))
+            return
+        if step == 1:
+            hop(q, n, side, 0).wait_recv()
+            onward(q, n, side, (1, 2))
+
+        @pl.when(z >= step)
+        def _():
+            for slot in (ex - 2 * step, side - 2 * step):
+                hop(q, n, slot, 0).wait_recv()
+                onward(q, n, slot, (1,))
+
+        @pl.when(z + step < line)
+        def _():
+            for slot in (ex + 2 * step, side + 2 * step):
+                hop(q, n, slot, 0).wait_recv()
+                onward(q, n, slot, (2,))
+
+    def by_both(q, n):
+        return line > 1 and (q, n) == (1, 2)
+
+    def relay(q, step, which=(0, 1, 2)):
+        for n in which:
+            if by_both(q, n):
+                relay_both(q, n, step)
+                continue
             if step == 0:
                 if q:
                     first(q, n).wait_recv()
@@ -453,6 +491,8 @@
 
     def settle(q):
         for n in range(3):
+            if by_both(q, n):
+                continue
             for level in range(line):
                 hop(q, n, 2 * level + 1 - col, 0).wait_recv()
 
@@ -590,19 +630,25 @@
 
     steps = max(line - 1, 1)
     turns = [range(chunks * n // (steps + 1), chunks * (n + 1) // (steps + 1)) for n in range(steps + 1)]
+    early = (0, 1)
+    for q in early:
+        relay(q, 0)
     for c in turns[0]:
         turn(c)
     relay(order[0], 0)
     for i, q in enumerate(order):
-        if i + 1 < replicas:
+        if i + 1 < replicas and order[i + 1] not in early:
             relay(order[i + 1], 0)
         for step in range(1, line):
-            relay(q, step)
-            if not i:
-                for c in turns[step]:
-                    turn(c)
-            if i:
-                pieces(local * (step - 1) // steps, local * step // steps, order[i - 1])
+            for part_of, which in enumerate(((0, 1), (2,))):
+                relay(q, step, which)
+                n = 2 * (step - 1) + part_of
+                if i:
+                    pieces(local * n // (2 * steps), local * (n + 1) // (2 * steps), order[i - 1])
+                else:
+                    mid = (len(turns[step]) + 1) // 2
+                    for c in turns[step][mid:] if part_of else turns[step][:mid]:
+                        turn(c)
         settle(q)
         prepare(q)
 
@@ -612,18 +658,24 @@
         finish(l)
 
     def sent_blocks(q, n):
+        both = by_both(q, n)
+        if both:
+            hop(q, n, ex, 0).wait_send()
+
         @pl.loop(0, line)
         def _(level):
-            slot = 2 * level + col
-            hop(q, n, slot, 0).wait_send()
-
-            @pl.when(above & (level <= z))
-            def _():
-                hop(q, n, slot, 1).wait_send()
-
-            @pl.when(below & (level >= z))
-            def _():
-                hop(q, n, slot, 2).wait_send()
+            for column in (col, 1 - col) if both else (col,):
+                slot = 2 * level + column
+                if not both:
+                    hop(q, n, slot, 0).wait_send()
+
+                @pl.when(above & (level <= z))
+                def _():
+                    hop(q, n, slot, 1).wait_send()
+
+                @pl.when(below & (level >= z))
+                def _():
+                    hop(q, n, slot, 2).wait_send()
 
     def add_dx(l, q, total):
         hit = lax.broadcasted_iota(jnp.int32, (slots, sources * tok), 0).astype(F32)
@@ -691,8 +743,10 @@
     last = []
     for q in (2, 3):
         round_dx(q, q - 2)
-        last.append(pltpu.make_async_copy(gx.at[q], out_dx.at[:, q - 2], w_sem.at[q - 2]))
-        last[-1].start()
+        for away in range(sources):
+            block = gx.at[q, flip(ex, away)]
+            last.append(pltpu.make_async_copy(block, out_dx[away].at[q - 2], far_sem.at[q - 2, away]))
+            last[-1].start()
     for j in range(2):
         near.end(j)
     home_copy = pltpu.make_async_copy(near.home, out_home, own_send.at[0, 0])
@@ -741,11 +795,10 @@
             jax.ShapeDtypeStruct((*rows, part), BF16),
             jax.ShapeDtypeStruct((*rows, 2 * ffn), BF16),
             jax.ShapeDtypeStruct((*rows, ffn), BF16),
-            jax.ShapeDtypeStruct((sources, 2, tok, part), BF16),
-            jax.ShapeDtypeStruct((2, tok, part), BF16),
+            *[jax.ShapeDtypeStruct((2, tok, part), BF16)] * (1 + sources),
         ),
         in_specs=[any_spec] * 4,
-        out_specs=(any_spec,) * 6,
+        out_specs=(any_spec,) * (5 + sources),
         scratch_shapes=[
             pltpu.VMEM((replicas, sources, tok, part), BF16),
             pltpu.VMEM((replicas, sources, tok, part), BF16),
@@ -772,6 +825,7 @@
             dma((3, local)),
             dma((2, replicas, local)),
             dma((2, ring)),
+            dma((2, sources)),
             *scatter_scratch(2, sources, tok, part),
         ],
         compiler_params=pltpu.CompilerParams(
@@ -904,17 +958,21 @@
         terms.append(head.astype(BF16))
         rest = rest - head
     at_once = 2 * replicas * sources * tok_dev * part + 20 * local * slots * kinds * ffn
-    if replicas == 4 and sources % 2 == 0 and at_once < 32 << 20:
+    if replicas == 4 and sources >= 2 and sources & (sources - 1) == 0 and at_once < 32 << 20:
         meta = jnp.concatenate(terms, axis=1)
         meta = jnp.pad(meta, ((0, -top % 16), (0, 0)))
-        *grown, dx, near = forward(inputs, out_grad, meta, weights, replicas, sources, CAP)
-        far = lax.psum_scatter(
-            dx.reshape(sources, 2 * tok_dev, part), "exp", scatter_dimension=0, tiled=False
-        )
-        far = [swap(far[j * tok_dev : (j + 1) * tok_dev], j + 2) for j in range(2)]
+        *grown, near, own_dx = (outs := forward(
+            inputs, out_grad, meta, weights, replicas, sources, CAP
+        ))[:6]
+        came = []
+        for away, block in enumerate(outs[6:], 1):
+            pairs = [(i, i ^ away) for i in range(sources)]
+            came.append(lax.ppermute(block, "exp", pairs))
         first_moment, second_moment, new_weights = expert_update(
             *grown, weights, moment_one, moment_two
         )
+        far = sum([block.astype(F32) for block in came], own_dx.astype(F32)).astype(BF16)
+        far = [swap(far[j], j + 2) for j in range(2)]
         home = jnp.concatenate([near, jnp.stack(far)])
     else:
         *grown, home = by_collectives(inputs, out_grad, terms, weights, top, sources, swap)

time: 336 us -> 303 us (0.902)
  the two profiles are of different devices: /device:TPU:1 before, /device:TPU:17 now
where the time goes in v2:
time: 303 us; the launch traced here: 302 us
  Pallas kernels  242 us (80%)
  waiting for transfers between devices  44.7 us (15%)
  starting transfers between devices  10.6 us (3%)
  other arithmetic  4.13 us (1%)
    pallas_call x1, Pallas kernels, forward(): pl.pallas_call(functools.partial(forward_kernel, dims), out_shape=(jax.Sh...  192 us
    pallas_call x1, Pallas kernels, expert_update(): pl.pallas_call(kernel, out_shape=out_shape, in_specs=[any_spec] * (len(pi...  49.9 us
    ppermute x7, waiting for transfers between devices, per_device(): came.append(lax.ppermute(block, 'exp', pairs))  44.7 us
    ppermute x7, starting transfers between devices, per_device(): came.append(lax.ppermute(block, 'exp', pairs))  6.74 us
  transfers between devices with their start and end apart: 9, of which 6 were waited for; matrix products, arithmetic and copies ran while one was open for 0% of the time, Pallas kernels for 17%

profile of v2, /device:TPU:17, one launch (start us, length us, event | category | flops | bytes accessed | tf_op | source)
XLA Modules:
  0.0 302.1 jit_solution(10986423768203465963)
XLA Ops:
  0.6 0.7 convert_bitcast_fusion
  1.3 0.7 reduce-precision_convert_fusion.1
  2.0 0.6 fusion.6.meta
  2.6 191.9 %gather_forward.1 = (bf16[4,8,144,512]{3,2,1,0:T(8,128)(2,1)}, bf16[4,8,144,512]{3,2,1,0:T(8,128)(2,1)}, bf16[4,8,144,768]{3,2,1,0:T(8,128)(2,1)}, bf16[4,8,144,...) custom-call(bf16[128,2048]{1,0:T(8,128)(2,1)} %x.3, ...), custom_call_target="tpu_custom_call" | custom-call | tf_op jit(solution)/shard_map/gather_forward/pallas_call | solution.py:791
  194.6 1.3 collective-permute-start
  195.9 2.0 collective-permute-start.1
  197.8 0.0 collective-permute-start.2
  197.8 0.0 collective-permute-start.3
  197.8 3.3 %collective-permute-start.4 = (bf16[2,128,512]{2,1,0:T(8,128)(2,1)}, bf16[2,128,512]{2,1,0:T(8,128)(2,1)S(1)}, u32[]{:S(2)}, u32[]{:S(2)}) collective-permute-start(bf16[2,128,512]{2,1,0:T(8,128)(2,1)} %get-tuple-element.26), channel_id=1, source_target_pairs={{0,5},{1,4},{2,7},{3,6},{4,1},{5,0},{6,3},{7,2},{8,13},{9,12},{10,... | collective-permute-start | bytes 786440 | tf_op jit(solution)/shard_map/ppermute | solution.py:970
  201.1 1.1 collective-permute-done
  202.2 0.2 collective-permute-start.5
  202.4 8.9 %collective-permute-done.1 = bf16[2,128,512]{2,1,0:T(8,128)(2,1)S(1)} collective-permute-done((bf16[2,128,512]{2,1,0:T(8,128)(2,1)}, bf16[2,128,512]{2,1,0:T(8,128)(2,1)S(1)}, u32[]{:S(2)}, u32[]{:S(2)}) %collective-permute-start.1) | collective-permute-done | bytes 262176 | tf_op jit(solution)/shard_map/ppermute | solution.py:970
  211.2 0.0 collective-permute-start.6
  211.3 5.6 %collective-permute-done.2 = bf16[2,128,512]{2,1,0:T(8,128)(2,1)S(1)} collective-permute-done((bf16[2,128,512]{2,1,0:T(8,128)(2,1)}, bf16[2,128,512]{2,1,0:T(8,128)(2,1)S(1)}, u32[]{:S(2)}, u32[]{:S(2)}) %collective-permute-start.2) | collective-permute-done | bytes 262176 | tf_op jit(solution)/shard_map/ppermute | solution.py:970
  216.9 0.0 collective-permute-done.3
  216.9 3.0 %collective-permute-done.4 = bf16[2,128,512]{2,1,0:T(8,128)(2,1)S(1)} collective-permute-done((bf16[2,128,512]{2,1,0:T(8,128)(2,1)}, bf16[2,128,512]{2,1,0:T(8,128)(2,1)S(1)}, u32[]{:S(2)}, u32[]{:S(2)}) %collective-permute-start.4) | collective-permute-done | bytes 262176 | tf_op jit(solution)/shard_map/ppermute | solution.py:970
  219.9 19.7 %collective-permute-done.5 = bf16[2,128,512]{2,1,0:T(8,128)(2,1)S(1)} collective-permute-done((bf16[2,128,512]{2,1,0:T(8,128)(2,1)}, bf16[2,128,512]{2,1,0:T(8,128)(2,1)S(1)}, u32[]{:S(2)}, u32[]{:S(2)}) %collective-permute-start.5) | collective-permute-done | bytes 262176 | tf_op jit(solution)/shard_map/ppermute | solution.py:970
  239.6 6.4 %collective-permute-done.6 = bf16[2,128,512]{2,1,0:T(8,128)(2,1)S(1)} collective-permute-done((bf16[2,128,512]{2,1,0:T(8,128)(2,1)}, bf16[2,128,512]{2,1,0:T(8,128)(2,1)S(1)}, u32[]{:S(2)}, u32[]{:S(2)}) %collective-permute-start.6) | collective-permute-done | bytes 262176 | tf_op jit(solution)/shard_map/ppermute | solution.py:970
  246.0 1.2 add_convert_fusion
  247.3 1.3 collective-permute-start.7
  248.6 2.6 collective-permute-start.8
  251.2 0.0 copy-start
  251.2 49.9 %expert_update.1 = (f32[512,3,8,384]{3,2,1,0:T(8,128)}, f32[512,3,8,384]{3,2,1,0:T(8,128)}, bf16[512,3,8,384]{3,2,1,0:T(8,128)(2,1)}) custom-call(bf16[4,8,144,512]{3,2,1,0:T(8,128)(2,1)} %get-tuple-element.29.refs_0_, bf16[4,8,144,512]{3,2,1,0:T(8,128)(2,1)} %get-tuple-element.30.refs_1_, bf16[4,8,144,768]{3,2,1,0:T(8,128)(2,1)} %get-tuple-element.31.refs_2_, ...), custom_call_target="tpu_custom_call" | custom-call | flops 5435817984 | bytes 94371840 | tf_op jit(solution)/shard_map/expert_update/pallas_call | solution.py:294
  301.1 0.0 collective-permute-done.7
  301.1 0.0 collective-permute-done.8
  301.1 0.0 copy-done
  301.2 0.1 pad_maximum_fusion
  301.3 0.8 pad_maximum_fusion.1
  (2 shorter events, 0.1 us)
Async XLA Ops:
  194.6 7.6 %collective-permute-start = (bf16[2,128,512]{2,1,0:T(8,128)(2,1)}, bf16[2,128,512]{2,1,0:T(8,128)(2,1)S(1)}, u32[]{:S(2)}, u32[]{:S(2)}) collective-permute-start(bf16[2,128,512]{2,1,0:T(8,128)(2,1)} %get-tuple-element.22), channel_id=1, source_target_pairs={{0,1},{1,0},{2,3},{3,2},{4,5},{5,4},{6,7},{7,6},{8,9},{9,8},{10,11... | collective-permute-start | bytes 786440 | tf_op jit(solution)/shard_map/ppermute | solution.py:970
  195.9 15.4 %collective-permute-start.1 = (bf16[2,128,512]{2,1,0:T(8,128)(2,1)}, bf16[2,128,512]{2,1,0:T(8,128)(2,1)S(1)}, u32[]{:S(2)}, u32[]{:S(2)}) collective-permute-start(bf16[2,128,512]{2,1,0:T(8,128)(2,1)} %get-tuple-element.23), channel_id=1, source_target_pairs={{0,2},{1,3},{2,0},{3,1},{4,6},{5,7},{6,4},{7,5},{8,10},{9,11},{10,... | collective-permute-start | bytes 786440 | tf_op jit(solution)/shard_map/ppermute | solution.py:970
  197.8 19.0 %collective-permute-start.2 = (bf16[2,128,512]{2,1,0:T(8,128)(2,1)}, bf16[2,128,512]{2,1,0:T(8,128)(2,1)S(1)}, u32[]{:S(2)}, u32[]{:S(2)}) collective-permute-start(bf16[2,128,512]{2,1,0:T(8,128)(2,1)} %get-tuple-element.24), channel_id=1, source_target_pairs={{0,3},{1,2},{2,1},{3,0},{4,7},{5,6},{6,5},{7,4},{8,11},{9,10},{10,... | collective-permute-start | bytes 786440 | tf_op jit(solution)/shard_map/ppermute | solution.py:970
  197.8 19.0 %collective-permute-start.3 = (bf16[2,128,512]{2,1,0:T(8,128)(2,1)}, bf16[2,128,512]{2,1,0:T(8,128)(2,1)S(1)}, u32[]{:S(2)}, u32[]{:S(2)}) collective-permute-start(bf16[2,128,512]{2,1,0:T(8,128)(2,1)} %get-tuple-element.25), channel_id=1, source_target_pairs={{0,4},{1,5},{2,6},{3,7},{4,0},{5,1},{6,2},{7,3},{8,12},{9,13},{10,... | collective-permute-start | bytes 786440 | tf_op jit(solution)/shard_map/ppermute | solution.py:970
  197.8 22.1 %collective-permute-start.4 = (bf16[2,128,512]{2,1,0:T(8,128)(2,1)}, bf16[2,128,512]{2,1,0:T(8,128)(2,1)S(1)}, u32[]{:S(2)}, u32[]{:S(2)}) collective-permute-start(bf16[2,128,512]{2,1,0:T(8,128)(2,1)} %get-tuple-element.26), channel_id=1, source_target_pairs={{0,5},{1,4},{2,7},{3,6},{4,1},{5,0},{6,3},{7,2},{8,13},{9,12},{10,... | collective-permute-start | bytes 786440 | tf_op jit(solution)/shard_map/ppermute | solution.py:970
  202.2 37.4 %collective-permute-start.5 = (bf16[2,128,512]{2,1,0:T(8,128)(2,1)}, bf16[2,128,512]{2,1,0:T(8,128)(2,1)S(1)}, u32[]{:S(2)}, u32[]{:S(2)}) collective-permute-start(bf16[2,128,512]{2,1,0:T(8,128)(2,1)} %get-tuple-element.27), channel_id=1, source_target_pairs={{0,6},{1,7},{2,4},{3,5},{4,2},{5,3},{6,0},{7,1},{8,14},{9,15},{10,... | collective-permute-start | bytes 786440 | tf_op jit(solution)/shard_map/ppermute | solution.py:970
  211.2 34.8 %collective-permute-start.6 = (bf16[2,128,512]{2,1,0:T(8,128)(2,1)}, bf16[2,128,512]{2,1,0:T(8,128)(2,1)S(1)}, u32[]{:S(2)}, u32[]{:S(2)}) collective-permute-start(bf16[2,128,512]{2,1,0:T(8,128)(2,1)} %get-tuple-element.28), channel_id=1, source_target_pairs={{0,7},{1,6},{2,5},{3,4},{4,3},{5,2},{6,1},{7,0},{8,15},{9,14},{10,... | collective-permute-start | bytes 786440 | tf_op jit(solution)/shard_map/ppermute | solution.py:970
  247.3 53.8 %collective-permute-start.7 = (bf16[128,512]{1,0:T(8,128)(2,1)S(1)}, bf16[128,512]{1,0:T(8,128)(2,1)S(1)}, u32[]{:S(2)}, u32[]{:S(2)}) collective-permute-start(bf16[128,512]{1,0:T(8,128)(2,1)S(1)} %get-tuple-element.40), channel_id=1, source_target_pairs={{0,16},{8,24},{16,0},{24,8},{1,17},{9,25},{17,1},{25,9},{2,18},{10... | collective-permute-start | bytes 393224 | tf_op jit(solution)/shard_map/ppermute | solution.py:953
  248.6 52.6 %collective-permute-start.8 = (bf16[128,512]{1,0:T(8,128)(2,1)S(1)}, bf16[128,512]{1,0:T(8,128)(2,1)S(1)}, u32[]{:S(2)}, u32[]{:S(2)}) collective-permute-start(bf16[128,512]{1,0:T(8,128)(2,1)S(1)} %get-tuple-element.41), channel_id=1, source_target_pairs={{0,24},{8,16},{16,8},{24,0},{1,25},{9,17},{17,9},{25,1},{2,26},{10... | collective-permute-start | bytes 393224 | tf_op jit(solution)/shard_map/ppermute | solution.py:953
  251.2 50.0 %copy-start = (bf16[2,128,512]{2,1,0:T(8,128)(2,1)S(1)}, bf16[2,128,512]{2,1,0:T(8,128)(2,1)}, u32[]{:S(2)}) copy-start(bf16[2,128,512]{2,1,0:T(8,128)(2,1)} %get-tuple-element.20) | copy-start | bytes 786436

commit v3 on v2

--- a/solution.py
+++ b/solution.py
@@ -677,18 +677,28 @@
                 def _():
                     hop(q, n, slot, 2).wait_send()
 
-    def add_dx(l, q, total):
-        hit = lax.broadcasted_iota(jnp.int32, (slots, sources * tok), 0).astype(F32)
-        pick = jnp.where(hit == rank[q, pl.ds(l, 1), :], 1.0, 0.0).astype(BF16)
-        slot_dx = lax.dot_general(
-            held[q, l, :, :pair],
-            w[l, :, :pair],
-            (((1,), (1,)), ((), ())),
+    def add_dx(l, q, total, count):
+        index = lax.broadcasted_iota(jnp.int32, (slots, sources * tok), 0).astype(F32)
+        picks, terms = [], []
+        for more in range(count):
+            hit = index == rank[q, pl.ds(l + more, 1), :]
+            picks.append(jnp.where(hit, 1.0, 0.0).astype(BF16))
+            slot_dx = lax.dot_general(
+                held[q, l + more, :, :pair],
+                w[l + more, :, :pair],
+                (((1,), (1,)), ((), ())),
+                preferred_element_type=F32,
+            )
+            terms.append(slot_dx.astype(BF16))
+        sum_dx[total] += lax.dot_general(
+            jnp.concatenate(picks, axis=0),
+            jnp.concatenate(terms, axis=0),
+            (((0,), (0,)), ((), ())),
             preferred_element_type=F32,
-        ).astype(BF16)
-        sum_dx[total] += lax.dot_general(
-            pick, slot_dx, (((0,), (0,)), ((), ())), preferred_element_type=F32
-        )
+        )
+
+    few = 2 if local % 2 == 0 else 1
+    many = 4 if local % 4 == 0 else few
 
     def round_dx(q, total):
         sent_blocks(q, 1)
@@ -703,9 +713,9 @@
     )
     sum_dx[...] = jnp.zeros_like(sum_dx)
 
-    @pl.loop(0, local)
-    def _(l):
-        add_dx(l, 0, 0)
+    @pl.loop(0, local // many)
+    def _(n):
+        add_dx(n * many, 0, 0, many)
 
     round_dx(0, 0)
     near.begin(0)
@@ -715,7 +725,10 @@
         grads_to(l, 0).wait_recv()
         for copy in d_out(l, 1):
             copy.start()
-        add_dx(l, 1, 1)
+
+    @pl.loop(0, local // many)
+    def _(n):
+        add_dx(n * many, 1, 1, many)
 
     round_dx(1, 1)
     near.begin(1)
@@ -726,19 +739,22 @@
     for j in range(2):
         near.finish(j)
 
-    @pl.loop(0, local + 1)
-    def _(l):
-        @pl.when(l < local)
+    @pl.loop(0, local // few + 1)
+    def _(n):
+        @pl.when(n < local // few)
         def _():
-            pass_on(l)
-            add_dx(l, 2, 0)
-
-        @pl.when(l >= 1)
+            for more in range(few):
+                pass_on(n * few + more)
+            add_dx(n * few, 2, 0, few)
+
+        @pl.when(n >= 1)
         def _():
-            grads_to(l - 1, 2).wait_recv()
-            for copy in d_out(l - 1, 3):
-                copy.start()
-            add_dx(l - 1, 3, 1)
+            for more in range(few):
+                l = (n - 1) * few + more
+                grads_to(l, 2).wait_recv()
+                for copy in d_out(l, 3):
+                    copy.start()
+            add_dx((n - 1) * few, 3, 1, few)
 
     last = []
     for q in (2, 3):

time: 303 us -> 303 us (level)
  transfers between devices with their start and end apart: 9 -> 9, of which waited for: 6 -> 5; matrix products, arithmetic and copies ran while one was open for 0% -> 0% of each run, Pallas kernels for 17% -> 16%
where the time goes in v3:
time: 303 us
  Pallas kernels  242 us (80%)
  waiting for transfers between devices  43.4 us (14%)
  starting transfers between devices  12 us (4%)
  other arithmetic  4.13 us (1%)
    pallas_call x1, Pallas kernels, forward(): pl.pallas_call(functools.partial(forward_kernel, dims), out_shape=(jax.Sh...  192 us
    pallas_call x1, Pallas kernels, expert_update(): pl.pallas_call(kernel, out_shape=out_shape, in_specs=[any_spec] * (len(pi...  49.9 us
    ppermute x7, waiting for transfers between devices, per_device(): came.append(lax.ppermute(block, 'exp', pairs))  43.4 us
    ppermute x7, starting transfers between devices, per_device(): came.append(lax.ppermute(block, 'exp', pairs))  6.78 us
  transfers between devices with their start and end apart: 9, of which 5 were waited for; matrix products, arithmetic and copies ran while one was open for 0% of the time, Pallas kernels for 16%

profile of v3, /device:TPU:17, one launch (start us, length us, event | category | flops | bytes accessed | tf_op | source)
XLA Modules:
  0.0 302.7 jit_solution(16761998138134691767)
XLA Ops:
  0.6 0.7 convert_bitcast_fusion
  1.3 0.7 reduce-precision_convert_fusion.1
  2.0 0.6 fusion.6.meta
  2.6 192.4 %gather_forward.1 = (bf16[4,8,144,512]{3,2,1,0:T(8,128)(2,1)}, bf16[4,8,144,512]{3,2,1,0:T(8,128)(2,1)}, bf16[4,8,144,768]{3,2,1,0:T(8,128)(2,1)}, bf16[4,8,144,...) custom-call(bf16[128,2048]{1,0:T(8,128)(2,1)} %x.3, ...), custom_call_target="tpu_custom_call" | custom-call | tf_op jit(solution)/shard_map/gather_forward/pallas_call | solution.py:807
  195.1 1.3 collective-permute-start
  196.4 2.0 collective-permute-start.1
  198.4 0.0 collective-permute-start.2
  198.4 0.0 collective-permute-start.3
  198.4 3.3 %collective-permute-start.4 = (bf16[2,128,512]{2,1,0:T(8,128)(2,1)}, bf16[2,128,512]{2,1,0:T(8,128)(2,1)S(1)}, u32[]{:S(2)}, u32[]{:S(2)}) collective-permute-start(bf16[2,128,512]{2,1,0:T(8,128)(2,1)} %get-tuple-element.26), channel_id=1, source_target_pairs={{0,5},{1,4},{2,7},{3,6},{4,1},{5,0},{6,3},{7,2},{8,13},{9,12},{10,... | collective-permute-start | bytes 786440 | tf_op jit(solution)/shard_map/ppermute | solution.py:986
  201.6 0.0 collective-permute-done
  201.7 0.2 collective-permute-start.5
  201.9 7.1 %collective-permute-done.1 = bf16[2,128,512]{2,1,0:T(8,128)(2,1)S(1)} collective-permute-done((bf16[2,128,512]{2,1,0:T(8,128)(2,1)}, bf16[2,128,512]{2,1,0:T(8,128)(2,1)S(1)}, u32[]{:S(2)}, u32[]{:S(2)}) %collective-permute-start.1) | collective-permute-done | bytes 262176 | tf_op jit(solution)/shard_map/ppermute | solution.py:986
  209.0 0.0 collective-permute-start.6
  209.0 7.3 %collective-permute-done.2 = bf16[2,128,512]{2,1,0:T(8,128)(2,1)S(1)} collective-permute-done((bf16[2,128,512]{2,1,0:T(8,128)(2,1)}, bf16[2,128,512]{2,1,0:T(8,128)(2,1)S(1)}, u32[]{:S(2)}, u32[]{:S(2)}) %collective-permute-start.2) | collective-permute-done | bytes 262176 | tf_op jit(solution)/shard_map/ppermute | solution.py:986
  216.4 0.0 collective-permute-done.3
  216.4 3.0 collective-permute-done.4
  219.4 19.7 %collective-permute-done.5 = bf16[2,128,512]{2,1,0:T(8,128)(2,1)S(1)} collective-permute-done((bf16[2,128,512]{2,1,0:T(8,128)(2,1)}, bf16[2,128,512]{2,1,0:T(8,128)(2,1)S(1)}, u32[]{:S(2)}, u32[]{:S(2)}) %collective-permute-start.5) | collective-permute-done | bytes 262176 | tf_op jit(solution)/shard_map/ppermute | solution.py:986
  239.1 6.1 %collective-permute-done.6 = bf16[2,128,512]{2,1,0:T(8,128)(2,1)S(1)} collective-permute-done((bf16[2,128,512]{2,1,0:T(8,128)(2,1)}, bf16[2,128,512]{2,1,0:T(8,128)(2,1)S(1)}, u32[]{:S(2)}, u32[]{:S(2)}) %collective-permute-start.6) | collective-permute-done | bytes 262176 | tf_op jit(solution)/shard_map/ppermute | solution.py:986
  245.2 1.2 add_convert_fusion
  246.5 1.5 collective-permute-start.7
  248.0 3.6 %collective-permute-start.8 = (bf16[128,512]{1,0:T(8,128)(2,1)S(1)}, bf16[128,512]{1,0:T(8,128)(2,1)S(1)}, u32[]{:S(2)}, u32[]{:S(2)}) collective-permute-start(bf16[128,512]{1,0:T(8,128)(2,1)S(1)} %get-tuple-element.41), channel_id=1, source_target_pairs={{0,24},{8,16},{16,8},{24,0},{1,25},{9,17},{17,9},{25,1},{2,26},{10... | collective-permute-start | bytes 393224 | tf_op jit(solution)/shard_map/ppermute | solution.py:969
  251.7 0.0 copy-start
  251.7 49.9 %expert_update.1 = (f32[512,3,8,384]{3,2,1,0:T(8,128)}, f32[512,3,8,384]{3,2,1,0:T(8,128)}, bf16[512,3,8,384]{3,2,1,0:T(8,128)(2,1)}) custom-call(bf16[4,8,144,512]{3,2,1,0:T(8,128)(2,1)} %get-tuple-element.29.refs_0_, bf16[4,8,144,512]{3,2,1,0:T(8,128)(2,1)} %get-tuple-element.30.refs_1_, bf16[4,8,144,768]{3,2,1,0:T(8,128)(2,1)} %get-tuple-element.31.refs_2_, ...), custom_call_target="tpu_custom_call" | custom-call | flops 5435817984 | bytes 94371840 | tf_op jit(solution)/shard_map/expert_update/pallas_call | solution.py:294
  301.6 0.0 collective-permute-done.7
  301.7 0.0 collective-permute-done.8
  301.7 0.0 copy-done
  301.7 0.1 pad_maximum_fusion
  301.8 0.8 pad_maximum_fusion.1
  (2 shorter events, 0.1 us)
Async XLA Ops:
  195.1 6.6 %collective-permute-start = (bf16[2,128,512]{2,1,0:T(8,128)(2,1)}, bf16[2,128,512]{2,1,0:T(8,128)(2,1)S(1)}, u32[]{:S(2)}, u32[]{:S(2)}) collective-permute-start(bf16[2,128,512]{2,1,0:T(8,128)(2,1)} %get-tuple-element.22), channel_id=1, source_target_pairs={{0,1},{1,0},{2,3},{3,2},{4,5},{5,4},{6,7},{7,6},{8,9},{9,8},{10,11... | collective-permute-start | bytes 786440 | tf_op jit(solution)/shard_map/ppermute | solution.py:986
  196.4 12.6 %collective-permute-start.1 = (bf16[2,128,512]{2,1,0:T(8,128)(2,1)}, bf16[2,128,512]{2,1,0:T(8,128)(2,1)S(1)}, u32[]{:S(2)}, u32[]{:S(2)}) collective-permute-start(bf16[2,128,512]{2,1,0:T(8,128)(2,1)} %get-tuple-element.23), channel_id=1, source_target_pairs={{0,2},{1,3},{2,0},{3,1},{4,6},{5,7},{6,4},{7,5},{8,10},{9,11},{10,... | collective-permute-start | bytes 786440 | tf_op jit(solution)/shard_map/ppermute | solution.py:986
  198.4 18.0 %collective-permute-start.2 = (bf16[2,128,512]{2,1,0:T(8,128)(2,1)}, bf16[2,128,512]{2,1,0:T(8,128)(2,1)S(1)}, u32[]{:S(2)}, u32[]{:S(2)}) collective-permute-start(bf16[2,128,512]{2,1,0:T(8,128)(2,1)} %get-tuple-element.24), channel_id=1, source_target_pairs={{0,3},{1,2},{2,1},{3,0},{4,7},{5,6},{6,5},{7,4},{8,11},{9,10},{10,... | collective-permute-start | bytes 786440 | tf_op jit(solution)/shard_map/ppermute | solution.py:986
  198.4 18.0 %collective-permute-start.3 = (bf16[2,128,512]{2,1,0:T(8,128)(2,1)}, bf16[2,128,512]{2,1,0:T(8,128)(2,1)S(1)}, u32[]{:S(2)}, u32[]{:S(2)}) collective-permute-start(bf16[2,128,512]{2,1,0:T(8,128)(2,1)} %get-tuple-element.25), channel_id=1, source_target_pairs={{0,4},{1,5},{2,6},{3,7},{4,0},{5,1},{6,2},{7,3},{8,12},{9,13},{10,... | collective-permute-start | bytes 786440 | tf_op jit(solution)/shard_map/ppermute | solution.py:986
  198.4 21.0 %collective-permute-start.4 = (bf16[2,128,512]{2,1,0:T(8,128)(2,1)}, bf16[2,128,512]{2,1,0:T(8,128)(2,1)S(1)}, u32[]{:S(2)}, u32[]{:S(2)}) collective-permute-start(bf16[2,128,512]{2,1,0:T(8,128)(2,1)} %get-tuple-element.26), channel_id=1, source_target_pairs={{0,5},{1,4},{2,7},{3,6},{4,1},{5,0},{6,3},{7,2},{8,13},{9,12},{10,... | collective-permute-start | bytes 786440 | tf_op jit(solution)/shard_map/ppermute | solution.py:986
  201.7 37.4 %collective-permute-start.5 = (bf16[2,128,512]{2,1,0:T(8,128)(2,1)}, bf16[2,128,512]{2,1,0:T(8,128)(2,1)S(1)}, u32[]{:S(2)}, u32[]{:S(2)}) collective-permute-start(bf16[2,128,512]{2,1,0:T(8,128)(2,1)} %get-tuple-element.27), channel_id=1, source_target_pairs={{0,6},{1,7},{2,4},{3,5},{4,2},{5,3},{6,0},{7,1},{8,14},{9,15},{10,... | collective-permute-start | bytes 786440 | tf_op jit(solution)/shard_map/ppermute | solution.py:986
  209.0 36.2 %collective-permute-start.6 = (bf16[2,128,512]{2,1,0:T(8,128)(2,1)}, bf16[2,128,512]{2,1,0:T(8,128)(2,1)S(1)}, u32[]{:S(2)}, u32[]{:S(2)}) collective-permute-start(bf16[2,128,512]{2,1,0:T(8,128)(2,1)} %get-tuple-element.28), channel_id=1, source_target_pairs={{0,7},{1,6},{2,5},{3,4},{4,3},{5,2},{6,1},{7,0},{8,15},{9,14},{10,... | collective-permute-start | bytes 786440 | tf_op jit(solution)/shard_map/ppermute | solution.py:986
  246.5 55.2 %collective-permute-start.7 = (bf16[128,512]{1,0:T(8,128)(2,1)S(1)}, bf16[128,512]{1,0:T(8,128)(2,1)S(1)}, u32[]{:S(2)}, u32[]{:S(2)}) collective-permute-start(bf16[128,512]{1,0:T(8,128)(2,1)S(1)} %get-tuple-element.40), channel_id=1, source_target_pairs={{0,16},{8,24},{16,0},{24,8},{1,17},{9,25},{17,1},{25,9},{2,18},{10... | collective-permute-start | bytes 393224 | tf_op jit(solution)/shard_map/ppermute | solution.py:969
  248.0 53.6 %collective-permute-start.8 = (bf16[128,512]{1,0:T(8,128)(2,1)S(1)}, bf16[128,512]{1,0:T(8,128)(2,1)S(1)}, u32[]{:S(2)}, u32[]{:S(2)}) collective-permute-start(bf16[128,512]{1,0:T(8,128)(2,1)S(1)} %get-tuple-element.41), channel_id=1, source_target_pairs={{0,24},{8,16},{16,8},{24,0},{1,25},{9,17},{17,9},{25,1},{2,26},{10... | collective-permute-start | bytes 393224 | tf_op jit(solution)/shard_map/ppermute | solution.py:969
  251.7 50.0 %copy-start = (bf16[2,128,512]{2,1,0:T(8,128)(2,1)S(1)}, bf16[2,128,512]{2,1,0:T(8,128)(2,1)}, u32[]{:S(2)}) copy-start(bf16[2,128,512]{2,1,0:T(8,128)(2,1)} %get-tuple-element.20) | copy-start | bytes 786436
